TPU v7x, 256 devices: a whole 4x4x8 slice. The times are simulated.
256 devices in a mesh: gx: 32 (over y, z_lo, core), gy: 8 (over x, z_hi).
Axes of the slice: x: 4, y: 4, z: 8 (z_hi: 2, z_lo: 4; z = z_hi * 4 + z_lo), core: 2. Of those that a mesh axis runs over, the one named last changes fastest.
Arguments:
- solution_vector: float32 [3, 512, 128, 128], P(None, 'gx', 'gy'), may hold values from -1 to 3, as said below
- insulator_marker: int32 [512, 128, 128], P('gx', 'gy'), may hold values 0 or 1
- electrode_marker: int32 [512, 128, 128], P('gx', 'gy'), may hold values 0 or 1
- impurity_zone_index: int32 [128, 32, 32], P('gx', 'gy'), may hold values from 0 to 3
- conductivity_category: int32 [128, 32, 32], P('gx', 'gy'), may hold values from 0 to 3
- warmth_rise: float32 [128, 32, 32], P('gx', 'gy'), may hold values from 0 to 2
Outputs:
- new_state: float32 [3, 512, 128, 128], P(None, 'gx', 'gy')
- new_temperature: float32 [128, 32, 32], P('gx', 'gy')
Inputs may be any that keep to these rules, and one draw needn't show every extreme that they name: `solution_vector`: channel 0 is the potential; channels 1 and 2 are the electron and hole densities, which are positive.
All inputs are finite; a program needn't handle non-finite values. No bound on the sum of `insulator_marker` or of `electrode_marker` on one device may be relied on, other than what follows from the above.
Results may differ from a plain program's by a relative error of at most 0.0003.
Values sent between devices are 32-bit elements; how exact they have to be, the bound alone decides.
A program may use at most 64 MiB of HBM per device.

v0:
```python
import jax
import jax.numpy as jnp
from jax import lax
from jax.sharding import PartitionSpec as P

COARSEN_RATIO = 4
NEWTON = 3
SWEEPS = 3


poisson_scale = 2.0
charge_scale = 4.0
clock_offset = 24.0
contact_bias = 0.25
heat_gain = 1.0
sink_rate = 0.3
speed_falloff = 0.5
dope_table = (-2.0, -0.5, 0.5, 2.0)
conduct_table = (0.5, 1.0, 2.0, 4.0)


def padded(shard, sides, width):
    edges = {}
    for axis, dim in sides:
        size, length = (lax.axis_size(axis), shard.shape[dim])
        up = [(i, (i + 1) % size) for i in range(size - 1)]
        last = lax.slice_in_dim(shard, length - width, length, axis=dim)
        first = lax.slice_in_dim(shard, 0, width, axis=dim)
        edges[dim] = (
            lax.ppermute(last, axis, up),
            lax.ppermute(first, axis, [(b, a) for a, b in up]),
        )
    done = []
    for _, dim in sides:
        low, high = edges[dim]
        around = [(width, width) if d in done else (0, 0) for d in range(shard.ndim)]
        shard = jnp.concatenate([jnp.pad(low, around), shard, jnp.pad(high, around)], axis=dim)
        done.append(dim)
    return shard


def extended(block, sides, width):
    for axis, dim in sides:
        count = lax.axis_size(axis)
        forward = [(i, i + 1) for i in range(count - 1)]
        backward = [(target, source) for source, target in forward]
        low = lax.ppermute(
            lax.slice_in_dim(block, block.shape[dim] - width, None, axis=dim), axis, forward
        )
        high = lax.ppermute(lax.slice_in_dim(block, 0, width, axis=dim), axis, backward)
        block = jnp.concatenate([low, block, high], axis=dim)
    return block


def bernoulli(value):
    tiny = jnp.abs(value) < 0.0001
    safe = jnp.where(tiny, 1.0, jnp.expm1(value))
    return jnp.where(tiny, 1.0 - 0.5 * value, value / safe)


def bernoulli_slope(value):
    tiny = jnp.abs(value) < 0.05
    safe = jnp.where(tiny, 1.0, jnp.expm1(value))
    exact = (safe - value * jnp.exp(value)) / (safe * safe)
    series = -0.5 + value / 6.0 - value * value * value / 180.0
    return jnp.where(tiny, series, exact)


def neighbours(framed_array):
    return [
        framed_array[..., 2:, 1:-1, 1:-1],
        framed_array[..., :-2, 1:-1, 1:-1],
        framed_array[..., 1:-1, 2:, 1:-1],
        framed_array[..., 1:-1, :-2, 1:-1],
        framed_array[..., 1:-1, 1:-1, 2:],
        framed_array[..., 1:-1, 1:-1, :-2],
    ]


def centre(framed_array):
    return framed_array[..., 1:-1, 1:-1, 1:-1]


def lookup(labels, table):
    result = jnp.zeros(labels.shape, jnp.float32)
    for level, amount in enumerate(table):
        result = result + jnp.where(labels == level, amount, 0.0)
    return result


def refine_warmth(coarse):
    lattice_span = coarse.shape
    spread = jnp.broadcast_to(
        coarse[:, None, :, None, :, None],
        (
            lattice_span[0],
            COARSEN_RATIO,
            lattice_span[1],
            COARSEN_RATIO,
            lattice_span[2],
            COARSEN_RATIO,
        ),
    )
    return spread.reshape(
        lattice_span[0] * COARSEN_RATIO,
        lattice_span[1] * COARSEN_RATIO,
        lattice_span[2] * COARSEN_RATIO,
    )


def restrict(fine):
    lattice_span = fine.shape
    blocks = fine.reshape(
        lattice_span[0] // COARSEN_RATIO,
        COARSEN_RATIO,
        lattice_span[1] // COARSEN_RATIO,
        COARSEN_RATIO,
        lattice_span[2] // COARSEN_RATIO,
        COARSEN_RATIO,
    )
    return jnp.mean(blocks, axis=(1, 3, 5))


def relax_weight(framed_array, warming_input, caloric_transfer):
    total = sum(neighbours(framed_array))
    return (warming_input + caloric_transfer * total) / (sink_rate + 6.0 * caloric_transfer)


def framed_layers(array):
    widths = [(0, 0)] * (array.ndim - 1) + [(1, 1)]
    return jnp.pad(array, widths)


def linearized_correction(
    framed_array,
    permittivity_framed,
    interior_frame_mask,
    impurity_profile,
    electrode_active,
    species_drift_speed,
):
    voltage_field = centre(framed_array[0])
    negative_density = centre(framed_array[1])
    positive_density = centre(framed_array[2])
    eps_here = centre(permittivity_framed)
    lap_sum = jnp.zeros_like(voltage_field)
    face_sum = jnp.zeros_like(voltage_field)
    negative_current = jnp.zeros_like(voltage_field)
    positive_current = jnp.zeros_like(voltage_field)
    negative_gradient = jnp.zeros_like(voltage_field)
    positive_gradient = jnp.zeros_like(voltage_field)
    backward_scharfetter = jnp.zeros_like(voltage_field)
    forward_scharfetter = jnp.zeros_like(voltage_field)
    ohmic_dissipation = jnp.zeros_like(voltage_field)
    parts = zip(
        neighbours(framed_array[0]),
        neighbours(framed_array[1]),
        neighbours(framed_array[2]),
        neighbours(permittivity_framed),
        neighbours(interior_frame_mask),
    )
    for pot_near, elec_near, hole_near, eps_near, weight in parts:
        drop = pot_near - voltage_field
        plus = bernoulli(drop)
        minus = bernoulli(-drop)
        slope_plus = bernoulli_slope(drop)
        slope_minus = bernoulli_slope(-drop)
        face = weight * 0.5 * (eps_here + eps_near)
        lap_sum = lap_sum + face * drop
        face_sum = face_sum + face
        elec_flow = weight * (elec_near * plus - negative_density * minus)
        hole_flow = weight * (hole_near * minus - positive_density * plus)
        negative_current = negative_current + elec_flow
        positive_current = positive_current + hole_flow
        ohmic_dissipation = ohmic_dissipation + (elec_flow - hole_flow) * (elec_flow - hole_flow)
        negative_gradient = negative_gradient + weight * (
            -elec_near * slope_plus - negative_density * slope_minus
        )
        positive_gradient = positive_gradient + weight * (
            hole_near * slope_minus + positive_density * slope_plus
        )
        backward_scharfetter = backward_scharfetter + weight * minus
        forward_scharfetter = forward_scharfetter + weight * plus
    denom = negative_density + positive_density + 2.0
    annihilation_rate = (negative_density * positive_density - 1.0) / denom
    negative_generation = (positive_density + 1.0) * (positive_density + 1.0) / (denom * denom)
    positive_generation = (negative_density + 1.0) * (negative_density + 1.0) / (denom * denom)
    res_psi = poisson_scale * lap_sum + charge_scale * (
        positive_density - negative_density + impurity_profile
    )
    negative_mismatch = species_drift_speed * negative_current - annihilation_rate
    positive_mismatch = species_drift_speed * positive_current - annihilation_rate
    blank_array = jnp.zeros_like(voltage_field)
    unit_array = jnp.ones_like(voltage_field)
    res_psi = jnp.where(electrode_active, voltage_field - contact_bias * impurity_profile, res_psi)
    negative_mismatch = jnp.where(electrode_active, negative_density - 1.0, negative_mismatch)
    positive_mismatch = jnp.where(electrode_active, positive_density - 1.0, positive_mismatch)
    mat_aa = jnp.where(electrode_active, unit_array, -poisson_scale * face_sum)
    mat_ab = jnp.where(electrode_active, blank_array, -charge_scale * unit_array)
    mat_ac = jnp.where(electrode_active, blank_array, charge_scale * unit_array)
    jacobian_entry_second_first = jnp.where(
        electrode_active, blank_array, species_drift_speed * negative_gradient
    )
    jacobian_entry_second_second = jnp.where(
        electrode_active,
        unit_array,
        -species_drift_speed * backward_scharfetter - negative_generation - clock_offset,
    )
    mat_bc = jnp.where(electrode_active, blank_array, -positive_generation)
    jacobian_entry_third_first = jnp.where(
        electrode_active, blank_array, species_drift_speed * positive_gradient
    )
    mat_cb = jnp.where(electrode_active, blank_array, -negative_generation)
    jacobian_entry_third_third = jnp.where(
        electrode_active,
        unit_array,
        -species_drift_speed * forward_scharfetter - positive_generation - clock_offset,
    )
    cof_aa = jacobian_entry_second_second * jacobian_entry_third_third - mat_bc * mat_cb
    cof_ab = (
        mat_bc * jacobian_entry_third_first
        - jacobian_entry_second_first * jacobian_entry_third_third
    )
    cof_ac = (
        jacobian_entry_second_first * mat_cb
        - jacobian_entry_second_second * jacobian_entry_third_first
    )
    determ = mat_aa * cof_aa + mat_ab * cof_ab + mat_ac * cof_ac
    step_psi = (
        cof_aa * res_psi
        + (mat_ac * mat_cb - mat_ab * jacobian_entry_third_third) * negative_mismatch
        + (mat_ab * mat_bc - mat_ac * jacobian_entry_second_second) * positive_mismatch
    ) / determ
    step_n = (
        cof_ab * res_psi
        + (mat_aa * jacobian_entry_third_third - mat_ac * jacobian_entry_third_first)
        * negative_mismatch
        + (mat_ac * jacobian_entry_second_first - mat_aa * mat_bc) * positive_mismatch
    ) / determ
    step_p = (
        cof_ac * res_psi
        + (mat_ab * jacobian_entry_third_first - mat_aa * mat_cb) * negative_mismatch
        + (mat_aa * jacobian_entry_second_second - mat_ab * jacobian_entry_second_first)
        * positive_mismatch
    ) / determ
    new_pot = voltage_field - step_psi
    new_elec = negative_density * jnp.exp(-step_n / negative_density)
    new_hole = positive_density * jnp.exp(-step_p / positive_density)
    warming_field = (
        0.5 * species_drift_speed * ohmic_dissipation / (negative_density + positive_density)
    )
    return (jnp.stack([new_pot, new_elec, new_hole], 0), warming_field)


def inside(count, position, devices):
    first = position * count - 1 + jnp.arange(count + 2, dtype=jnp.int32)
    return ((first >= 0) & (first < count * devices)).astype(jnp.float32)


def inside_wide(count, position, devices, margin):
    first = position * count - margin + jnp.arange(count + 2 * margin, dtype=jnp.int32)
    return ((first >= 0) & (first < count * devices)).astype(jnp.float32)


def per_device(
    solution_vector,
    insulator_marker,
    electrode_marker,
    impurity_zone_index,
    conductivity_category,
    warmth_rise,
):
    rows_x = solution_vector.shape[1]
    rows_y = solution_vector.shape[2]
    depth = solution_vector.shape[3]
    eps = jnp.where(insulator_marker == 1, 0.4, 1.0).astype(jnp.float32)
    valid_x = inside(rows_x, lax.axis_index("gx"), lax.axis_size("gx"))
    valid_y = inside(rows_y, lax.axis_index("gy"), lax.axis_size("gy"))
    valid_z = jnp.pad(jnp.ones((depth,), jnp.float32), 1)
    interior_frame_mask = valid_x[:, None, None] * valid_y[None, :, None] * valid_z[None, None, :]
    impurity_profile = refine_warmth(lookup(impurity_zone_index, dope_table))
    caloric_transfer = lookup(conductivity_category, conduct_table)
    electrode_active = electrode_marker == 1
    cells_x = warmth_rise.shape[0]
    cells_y = warmth_rise.shape[1]
    cell_mask_x = inside_wide(cells_x, lax.axis_index("gx"), lax.axis_size("gx"), SWEEPS)
    cell_mask_y = inside_wide(cells_y, lax.axis_index("gy"), lax.axis_size("gy"), SWEEPS)
    cell_mask = cell_mask_x[:, None, None] * cell_mask_y[None, :, None]
    for newton_step in range(NEWTON):
        pointwise_warmth = warmth_rise
        species_drift_speed = 1.0 / (1.0 + speed_falloff * refine_warmth(pointwise_warmth))
        stacked = jnp.concatenate([solution_vector, eps[None]], 0)
        padded_all = framed_layers(padded(stacked, (("gx", 1), ("gy", 2)), 1))
        framed_array = padded_all[:3]
        permittivity_framed = padded_all[3]
        solution_vector, warming_field = linearized_correction(
            framed_array,
            permittivity_framed,
            interior_frame_mask,
            impurity_profile,
            electrode_active,
            species_drift_speed,
        )
        warming_input = heat_gain * restrict(warming_field)
        packed = jnp.stack([warmth_rise, warming_input, caloric_transfer], 0)
        widened = extended(packed, (("gx", 1), ("gy", 2)), SWEEPS)
        temp_wide = widened[0]
        source_wide = widened[1]
        cond_wide = widened[2]
        mask_wide = cell_mask
        for sweep in range(SWEEPS):
            source_wide = source_wide[1:-1, 1:-1]
            cond_wide = cond_wide[1:-1, 1:-1]
            mask_wide = mask_wide[1:-1, 1:-1]
            temp_wide = relax_weight(framed_layers(temp_wide), source_wide, cond_wide) * mask_wide
        warmth_rise = temp_wide
    return (solution_vector, warmth_rise)


def solution(mesh):
    placed = (
        P(None, "gx", "gy", None),
        P("gx", "gy", None),
        P("gx", "gy", None),
        P("gx", "gy", None),
        P("gx", "gy", None),
        P("gx", "gy", None),
    )
    return jax.shard_map(
        per_device,
        mesh=mesh,
        in_specs=placed,
        out_specs=(P(None, "gx", "gy", None), P("gx", "gy", None)),
        check_vma=False,
    )
```

profile of v0, /device:TPU:14, one launch (start us, length us, event | category | flops | bytes accessed | tf_op | source)
XLA Modules:
  0.0 207.2 jit_solution(15436460498474987335)
XLA Ops:
  0.6 0.9 select_bitcast_fusion
  1.6 1.1 fusion.386
  2.6 9.4 %collective-permute-start.3 = (f32[4,16,1,128]{3,2,1,0:T(1,128)S(1)}, f32[4,16,1,128]{3,2,1,0:T(1,128)S(1)}, u32[]{:S(2)}, u32[]{:S(2)}) collective-permute-start(f32[4,16,1,128]{3,2,1,0:T(1,128)S(1)} %get-tuple-element.119), channel_id=1, source_target_pairs={{1,0},{2,1},{3,2},{4,3},{5,4},{6,5},{7,6},{9,8},{10,9},{11,10},{12... | collective-permute-start | bytes 98312 | tf_op jit(solution)/shard_map/ppermute | solution.py:31
  12.0 1.9 collective-permute-start
  14.7 3.8 %collective-permute-start.2 = (f32[4,1,16,128]{3,2,1,0:T(8,128)S(1)}, f32[4,1,16,128]{3,2,1,0:T(8,128)S(1)}, u32[]{:S(2)}, u32[]{:S(2)}) collective-permute-start(f32[4,1,16,128]{3,2,1,0:T(8,128)S(1)} %get-tuple-element.117), channel_id=1, source_target_pairs={{8,0},{16,8},{24,16},{32,24},{40,32},{48,40},{56,48},{64,56},{72,6... | collective-permute-start | bytes 98312 | tf_op jit(solution)/shard_map/ppermute | solution.py:31
  18.5 1.9 collective-permute-start.1
  23.1 2.6 %broadcast_in_dim.152 = f32[4,4,4,4,32,4]{5,4,3,2,1,0:T(8,128)} broadcast(f32[4,4,32]{2,1,0:T(4,128)S(1)} %add_divide_fusion.5), dimensions={0,2,4} | broadcast | bytes 133120 | tf_op jit(solution)/shard_map/broadcast_in_dim | solution.py:93
  25.7 4.9 %div.577 = f32[16,16,128]{2,1,0:T(8,128)S(1)} reshape(f32[4,4,4,4,32,4]{5,4,3,2,1,0:T(8,128)} %broadcast_in_dim.152) | data formatting | bytes 262144 | tf_op jit(solution)/shard_map/div | solution.py:291
  30.5 2.6 %broadcast_in_dim.158 = f32[4,4,4,4,32,4]{5,4,3,2,1,0:T(8,128)} broadcast(f32[4,4,32]{2,1,0:T(4,128)S(1)} %select_add_fusion), dimensions={0,2,4} | broadcast | bytes 133120 | tf_op jit(solution)/shard_map/broadcast_in_dim | solution.py:93
  33.1 4.9 %reshape.181 = f32[16,16,128]{2,1,0:T(8,128)S(1)} reshape(f32[4,4,4,4,32,4]{5,4,3,2,1,0:T(8,128)} %broadcast_in_dim.158) | data formatting | bytes 262144 | tf_op jit(solution)/shard_map/reshape | solution.py:104
  38.7 2.7 %multiply_divide_fusion.6 = (f32[16,16,128]{2,1,0:T(8,128)S(1)}, f32[16,16,128]{2,1,0:T(8,128)S(1)}, f32[16,16,128]{2,1,0:T(8,128)S(1)}, f32[16,16,128]{2,1,0:T(...) fusion(f32[16,16,128]{2,1,0:T(8,128)S(1)} %div.577, ...), kind=kLoop, calls=%fused_computation.706 | loop fusion | flops 5406720 | bytes 6160384 | tf_op jit(solution)/shard_map/div | solution.py:250
  41.4 5.7 %reshape.182 = f32[4,4,4,4,32,4]{5,4,3,2,1,0:T(8,128)} reshape(f32[16,16,128]{2,1,0:T(8,128)S(1)} %get-tuple-element.59) | data formatting | bytes 262144 | tf_op jit(solution)/shard_map/reshape | solution.py:113
  47.1 2.6 %reduce_sum.27 = f32[4,4,32]{2,1,0:T(4,128)S(1)} reduce(f32[4,4,4,4,32,4]{5,4,3,2,1,0:T(8,128)} %reshape.182, f32[]{:T(128)} %constant.150.clone.1), dimensions={1,3,5}, to_apply=%region_0.1 | reduce | flops 32256 | bytes 133124 | tf_op jit(solution)/shard_map/reduce_sum | solution.py:121
  49.8 6.3 %collective-permute-start.9 = (f32[3,3,4,32]{3,2,1,0:T(4,128)S(1)}, f32[3,3,4,32]{3,2,1,0:T(4,128)S(1)}, u32[]{:S(2)}, u32[]{:S(2)}) collective-permute-start(f32[3,3,4,32]{3,2,1,0:T(4,128)S(1)} %get-tuple-element.146), channel_id=1, source_target_pairs={{8,0},{16,8},{24,16},{32,24},{40,32},{48,40},{56,48},{64,56},{72,6... | collective-permute-start | bytes 13832 | tf_op jit(solution)/shard_map/ppermute | solution.py:50
  56.1 1.9 collective-permute-start.8
  58.1 4.5 %fusion.379 = (f32[1,16,16,128]{3,2,1,0:T(8,128)S(1)}, f32[16,16,128]{2,1,0:T(8,128)S(1)}, f32[16,16,128]{2,1,0:T(8,128)S(1)}, f32[16,16,128]{2,1,0:T(8,128)S(1)...) fusion(f32[18,18,130]{2,1,0:T(8,128)S(1)} %get-tuple-element.10, ...), kind=kLoop, calls=%fused_computation.746 | loop fusion | flops 14647296 | bytes 7897088 | tf_op jit(solution)/shard_map/stack | solution.py:252
  64.0 7.6 %collective-permute-start.11 = (f32[3,10,3,32]{3,2,1,0:T(4,128)S(1)}, f32[3,10,3,32]{3,2,1,0:T(4,128)S(1)}, u32[]{:S(2)}, u32[]{:S(2)}) collective-permute-start(f32[3,10,3,32]{3,2,1,0:T(4,128)S(1)} %get-tuple-element.140), channel_id=1, source_target_pairs={{1,0},{2,1},{3,2},{4,3},{5,4},{6,5},{7,6},{9,8},{10,9},{11,10},{12... | collective-permute-start | bytes 34568 | tf_op jit(solution)/shard_map/ppermute | solution.py:50
  71.5 2.2 %collective-permute-start.10 = (f32[3,10,3,32]{3,2,1,0:T(4,128)S(1)}, f32[3,10,3,32]{3,2,1,0:T(4,128)S(1)}, u32[]{:S(2)}, u32[]{:S(2)}) collective-permute-start(f32[3,10,3,32]{3,2,1,0:T(4,128)S(1)} %get-tuple-element.139), channel_id=1, source_target_pairs={{0,1},{1,2},{2,3},{3,4},{4,5},{5,6},{6,7},{8,9},{9,10},{10,11},{11... | collective-permute-start | bytes 34568 | tf_op jit(solution)/shard_map/ppermute | solution.py:47
  73.7 8.5 %collective-permute-start.7 = (f32[4,16,1,128]{3,2,1,0:T(1,128)S(1)}, f32[4,16,1,128]{3,2,1,0:T(1,128)S(1)}, u32[]{:S(2)}, u32[]{:S(2)}) collective-permute-start(f32[4,16,1,128]{3,2,1,0:T(1,128)S(1)} %get-tuple-element.115), channel_id=1, source_target_pairs={{1,0},{2,1},{3,2},{4,3},{5,4},{6,5},{7,6},{9,8},{10,9},{11,10},{12... | collective-permute-start | bytes 98312 | tf_op jit(solution)/shard_map/ppermute | solution.py:31
  82.2 1.9 collective-permute-start.4
  84.1 4.6 %collective-permute-start.6 = (f32[4,1,16,128]{3,2,1,0:T(8,128)S(1)}, f32[4,1,16,128]{3,2,1,0:T(8,128)S(1)}, u32[]{:S(2)}, u32[]{:S(2)}) collective-permute-start(f32[4,1,16,128]{3,2,1,0:T(8,128)S(1)} %get-tuple-element.113), channel_id=1, source_target_pairs={{8,0},{16,8},{24,16},{32,24},{40,32},{48,40},{56,48},{64,56},{72,6... | collective-permute-start | bytes 98312 | tf_op jit(solution)/shard_map/ppermute | solution.py:31
  88.8 2.1 %collective-permute-start.5 = (f32[4,1,16,128]{3,2,1,0:T(8,128)S(1)}, f32[4,1,16,128]{3,2,1,0:T(8,128)S(1)}, u32[]{:S(2)}, u32[]{:S(2)}) collective-permute-start(f32[4,1,16,128]{3,2,1,0:T(8,128)S(1)} %get-tuple-element.112), channel_id=1, source_target_pairs={{0,8},{8,16},{16,24},{24,32},{32,40},{40,48},{48,56},{56,64},{64,7... | collective-permute-start | bytes 98312 | tf_op jit(solution)/shard_map/ppermute | solution.py:30
  91.3 2.6 %broadcast_in_dim.160 = f32[4,4,4,4,32,4]{5,4,3,2,1,0:T(8,128)} broadcast(f32[4,4,32]{2,1,0:T(4,128)S(1)} %get-tuple-element.57), dimensions={0,2,4} | broadcast | bytes 133120 | tf_op jit(solution)/shard_map/broadcast_in_dim | solution.py:93
  93.9 4.9 %div.641 = f32[16,16,128]{2,1,0:T(8,128)S(1)} reshape(f32[4,4,4,4,32,4]{5,4,3,2,1,0:T(8,128)} %broadcast_in_dim.160) | data formatting | bytes 262144 | tf_op jit(solution)/shard_map/div | solution.py:291
  99.7 3.5 %fusion.378 = (f32[1,16,16,128]{3,2,1,0:T(8,128)S(1)}, f32[16,16,128]{2,1,0:T(8,128)S(1)}, f32[16,16,128]{2,1,0:T(8,128)S(1)}, f32[16,16,128]{2,1,0:T(8,128)S(1)...) fusion(pred[16,16,128]{2,1,0:T(8,128)(4,1)S(1)} %get-tuple-elem, ...), kind=kLoop, calls=%fused_computation.745 | loop fusion | flops 16187392 | bytes 7766016 | tf_op jit(solution)/shard_map/stack | solution.py:252
  104.0 6.5 %reshape.183 = f32[4,4,4,4,32,4]{5,4,3,2,1,0:T(8,128)} reshape(f32[16,16,128]{2,1,0:T(8,128)} %multiply_divide_fusion.3) | data formatting | bytes 262144 | tf_op jit(solution)/shard_map/reshape | solution.py:113
  110.5 2.6 %reduce_sum.28 = f32[4,4,32]{2,1,0:T(4,128)S(1)} reduce(f32[4,4,4,4,32,4]{5,4,3,2,1,0:T(8,128)} %reshape.183, f32[]{:T(128)} %constant.150.clone.1), dimensions={1,3,5}, to_apply=%region_1.2 | reduce | flops 32256 | bytes 133124 | tf_op jit(solution)/shard_map/reduce_sum | solution.py:121
  113.2 6.3 %collective-permute-start.17 = (f32[3,3,4,32]{3,2,1,0:T(4,128)S(1)}, f32[3,3,4,32]{3,2,1,0:T(4,128)S(1)}, u32[]{:S(2)}, u32[]{:S(2)}) collective-permute-start(f32[3,3,4,32]{3,2,1,0:T(4,128)S(1)} %get-tuple-element.144), channel_id=1, source_target_pairs={{8,0},{16,8},{24,16},{32,24},{40,32},{48,40},{56,48},{64,56},{72,6... | collective-permute-start | bytes 13832 | tf_op jit(solution)/shard_map/ppermute | solution.py:50
  119.5 1.9 collective-permute-start.16
  121.9 5.5 %collective-permute-done.16 = f32[3,3,4,32]{3,2,1,0:T(4,128)S(1)} collective-permute-done((f32[3,3,4,32]{3,2,1,0:T(4,128)S(1)}, f32[3,3,4,32]{3,2,1,0:T(4,128)S(1)}, u32[]{:S(2)}, u32[]{:S(2)}) %collective-permute-start.16) | collective-permute-done | bytes 4640 | tf_op jit(solution)/shard_map/ppermute | solution.py:47
  127.4 8.6 %collective-permute-start.19 = (f32[3,10,3,32]{3,2,1,0:T(4,128)S(1)}, f32[3,10,3,32]{3,2,1,0:T(4,128)S(1)}, u32[]{:S(2)}, u32[]{:S(2)}) collective-permute-start(f32[3,10,3,32]{3,2,1,0:T(4,128)S(1)} %get-tuple-element.138), channel_id=1, source_target_pairs={{1,0},{2,1},{3,2},{4,3},{5,4},{6,5},{7,6},{9,8},{10,9},{11,10},{12... | collective-permute-start | bytes 34568 | tf_op jit(solution)/shard_map/ppermute | solution.py:50
  136.1 1.9 collective-permute-start.18
  138.0 8.7 %collective-permute-start.15 = (f32[4,16,1,128]{3,2,1,0:T(1,128)S(1)}, f32[4,16,1,128]{3,2,1,0:T(1,128)S(1)}, u32[]{:S(2)}, u32[]{:S(2)}) collective-permute-start(f32[4,16,1,128]{3,2,1,0:T(1,128)S(1)} %get-tuple-element.111), channel_id=1, source_target_pairs={{1,0},{2,1},{3,2},{4,3},{5,4},{6,5},{7,6},{9,8},{10,9},{11,10},{12... | collective-permute-start | bytes 98312 | tf_op jit(solution)/shard_map/ppermute | solution.py:31
  146.8 1.9 collective-permute-start.12
  148.7 1.9 collective-permute-start.14
  150.6 2.6 %collective-permute-start.13 = (f32[4,1,16,128]{3,2,1,0:T(8,128)S(1)}, f32[4,1,16,128]{3,2,1,0:T(8,128)S(1)}, u32[]{:S(2)}, u32[]{:S(2)}) collective-permute-start(f32[4,1,16,128]{3,2,1,0:T(8,128)S(1)} %get-tuple-element.108), channel_id=1, source_target_pairs={{0,8},{8,16},{16,24},{24,32},{32,40},{40,48},{48,56},{56,64},{64,7... | collective-permute-start | bytes 98312 | tf_op jit(solution)/shard_map/ppermute | solution.py:30
  153.7 2.6 %broadcast_in_dim.161 = f32[4,4,4,4,32,4]{5,4,3,2,1,0:T(8,128)} broadcast(f32[4,4,32]{2,1,0:T(4,128)S(1)} %get-tuple-element.55), dimensions={0,2,4} | broadcast | bytes 133120 | tf_op jit(solution)/shard_map/broadcast_in_dim | solution.py:93
  156.3 4.9 %div.705 = f32[16,16,128]{2,1,0:T(8,128)S(1)} reshape(f32[4,4,4,4,32,4]{5,4,3,2,1,0:T(8,128)} %broadcast_in_dim.161) | data formatting | bytes 262144 | tf_op jit(solution)/shard_map/div | solution.py:291
  161.8 2.7 %multiply_divide_fusion = (f32[16,16,128]{2,1,0:T(8,128)S(1)}, f32[16,16,128]{2,1,0:T(8,128)S(1)}, f32[16,16,128]{2,1,0:T(8,128)S(1)}, f32[16,16,128]{2,1,0:T(8,...) fusion(f32[16,16,128]{2,1,0:T(8,128)S(1)} %div.705, ...), kind=kLoop, calls=%fused_computation.632 | loop fusion | flops 5406720 | bytes 6160384 | tf_op jit(solution)/shard_map/div | solution.py:250
  164.5 5.7 %reshape.184 = f32[4,4,4,4,32,4]{5,4,3,2,1,0:T(8,128)} reshape(f32[16,16,128]{2,1,0:T(8,128)S(1)} %get-tuple-element.2) | data formatting | bytes 262144 | tf_op jit(solution)/shard_map/reshape | solution.py:113
  170.2 2.6 %reduce_sum.29 = f32[4,4,32]{2,1,0:T(4,128)S(1)} reduce(f32[4,4,4,4,32,4]{5,4,3,2,1,0:T(8,128)} %reshape.184, f32[]{:T(128)} %constant.150.clone.1), dimensions={1,3,5}, to_apply=%region_2.3 | reduce | flops 32256 | bytes 133124 | tf_op jit(solution)/shard_map/reduce_sum | solution.py:121
  172.8 5.9 %collective-permute-start.21 = (f32[3,3,4,32]{3,2,1,0:T(4,128)S(1)}, f32[3,3,4,32]{3,2,1,0:T(4,128)S(1)}, u32[]{:S(2)}, u32[]{:S(2)}) collective-permute-start(f32[3,3,4,32]{3,2,1,0:T(4,128)S(1)} %get-tuple-element.142), channel_id=1, source_target_pairs={{8,0},{16,8},{24,16},{32,24},{40,32},{48,40},{56,48},{64,56},{72,6... | collective-permute-start | bytes 13832 | tf_op jit(solution)/shard_map/ppermute | solution.py:50
  178.7 1.9 collective-permute-start.20
  180.6 4.5 %fusion.377 = (f32[1,16,16,128]{3,2,1,0:T(8,128)S(1)}, f32[16,16,128]{2,1,0:T(8,128)S(1)}, f32[16,16,128]{2,1,0:T(8,128)S(1)}, f32[16,16,128]{2,1,0:T(8,128)S(1)...) fusion(pred[16,16,128]{2,1,0:T(8,128)(4,1)S(1)} %get-tuple-elem, ...), kind=kLoop, calls=%fused_computation.744 | loop fusion | flops 14614528 | bytes 7766016 | tf_op jit(solution)/shard_map/stack | solution.py:252
  185.4 1.0 collective-permute-done.20
  186.5 8.7 %collective-permute-start.23 = (f32[3,10,3,32]{3,2,1,0:T(4,128)S(1)}, f32[3,10,3,32]{3,2,1,0:T(4,128)S(1)}, u32[]{:S(2)}, u32[]{:S(2)}) collective-permute-start(f32[3,10,3,32]{3,2,1,0:T(4,128)S(1)} %get-tuple-element.136), channel_id=1, source_target_pairs={{1,0},{2,1},{3,2},{4,3},{5,4},{6,5},{7,6},{9,8},{10,9},{11,10},{12... | collective-permute-start | bytes 34568 | tf_op jit(solution)/shard_map/ppermute | solution.py:50
  195.3 1.9 collective-permute-start.22
  198.0 8.2 %collective-permute-done.22 = f32[3,10,3,32]{3,2,1,0:T(4,128)S(1)} collective-permute-done((f32[3,10,3,32]{3,2,1,0:T(4,128)S(1)}, f32[3,10,3,32]{3,2,1,0:T(4,128)S(1)}, u32[]{:S(2)}, u32[]{:S(2)}) %collective-permute-start.22) | collective-permute-done | bytes 11552 | tf_op jit(solution)/shard_map/ppermute | solution.py:47
  (87 shorter events, 11.4 us)
Async XLA Ops:
  2.6 35.4 %collective-permute-start.3 = (f32[4,16,1,128]{3,2,1,0:T(1,128)S(1)}, f32[4,16,1,128]{3,2,1,0:T(1,128)S(1)}, u32[]{:S(2)}, u32[]{:S(2)}) collective-permute-start(f32[4,16,1,128]{3,2,1,0:T(1,128)S(1)} %get-tuple-element.119), channel_id=1, source_target_pairs={{1,0},{2,1},{3,2},{4,3},{5,4},{6,5},{7,6},{9,8},{10,9},{11,10},{12... | collective-permute-start | bytes 98312 | tf_op jit(solution)/shard_map/ppermute | solution.py:31
  12.0 26.0 %collective-permute-start = (f32[4,16,1,128]{3,2,1,0:T(1,128)S(1)}, f32[4,16,1,128]{3,2,1,0:T(1,128)S(1)}, u32[]{:S(2)}, u32[]{:S(2)}) collective-permute-start(f32[4,16,1,128]{3,2,1,0:T(1,128)S(1)} %get-tuple-element.118), channel_id=1, source_target_pairs={{0,1},{1,2},{2,3},{3,4},{4,5},{5,6},{6,7},{8,9},{9,10},{10,11},{11... | collective-permute-start | bytes 98312 | tf_op jit(solution)/shard_map/ppermute | solution.py:30
  14.7 23.3 %collective-permute-start.2 = (f32[4,1,16,128]{3,2,1,0:T(8,128)S(1)}, f32[4,1,16,128]{3,2,1,0:T(8,128)S(1)}, u32[]{:S(2)}, u32[]{:S(2)}) collective-permute-start(f32[4,1,16,128]{3,2,1,0:T(8,128)S(1)} %get-tuple-element.117), channel_id=1, source_target_pairs={{8,0},{16,8},{24,16},{32,24},{40,32},{48,40},{56,48},{64,56},{72,6... | collective-permute-start | bytes 98312 | tf_op jit(solution)/shard_map/ppermute | solution.py:31
  18.5 19.6 %collective-permute-start.1 = (f32[4,1,16,128]{3,2,1,0:T(8,128)S(1)}, f32[4,1,16,128]{3,2,1,0:T(8,128)S(1)}, u32[]{:S(2)}, u32[]{:S(2)}) collective-permute-start(f32[4,1,16,128]{3,2,1,0:T(8,128)S(1)} %get-tuple-element.116), channel_id=1, source_target_pairs={{0,8},{8,16},{16,24},{24,32},{32,40},{40,48},{48,56},{56,64},{64,7... | collective-permute-start | bytes 98312 | tf_op jit(solution)/shard_map/ppermute | solution.py:30
  33.1 5.0 %copy-start = (f32[3,16,16,128]{3,2,1,0:T(8,128)S(1)}, f32[3,16,16,128]{3,2,1,0:T(8,128)}, u32[]{:S(2)}) copy-start(f32[3,16,16,128]{3,2,1,0:T(8,128)} %param.6) | copy-start | bytes 1179652
  47.1 2.6 %copy-start.1 = (f32[4,4,32]{2,1,0:T(4,128)S(1)}, f32[4,4,32]{2,1,0:T(4,128)}, u32[]{:S(2)}) copy-start(f32[4,4,32]{2,1,0:T(4,128)} %param.11) | copy-start | bytes 6148
  49.8 13.2 %collective-permute-start.9 = (f32[3,3,4,32]{3,2,1,0:T(4,128)S(1)}, f32[3,3,4,32]{3,2,1,0:T(4,128)S(1)}, u32[]{:S(2)}, u32[]{:S(2)}) collective-permute-start(f32[3,3,4,32]{3,2,1,0:T(4,128)S(1)} %get-tuple-element.146), channel_id=1, source_target_pairs={{8,0},{16,8},{24,16},{32,24},{40,32},{48,40},{56,48},{64,56},{72,6... | collective-permute-start | bytes 13832 | tf_op jit(solution)/shard_map/ppermute | solution.py:50
  56.1 7.8 %collective-permute-start.8 = (f32[3,3,4,32]{3,2,1,0:T(4,128)S(1)}, f32[3,3,4,32]{3,2,1,0:T(4,128)S(1)}, u32[]{:S(2)}, u32[]{:S(2)}) collective-permute-start(f32[3,3,4,32]{3,2,1,0:T(4,128)S(1)} %get-tuple-element.145), channel_id=1, source_target_pairs={{0,8},{8,16},{16,24},{24,32},{32,40},{40,48},{48,56},{56,64},{64,7... | collective-permute-start | bytes 13832 | tf_op jit(solution)/shard_map/ppermute | solution.py:47
  64.0 24.8 %collective-permute-start.11 = (f32[3,10,3,32]{3,2,1,0:T(4,128)S(1)}, f32[3,10,3,32]{3,2,1,0:T(4,128)S(1)}, u32[]{:S(2)}, u32[]{:S(2)}) collective-permute-start(f32[3,10,3,32]{3,2,1,0:T(4,128)S(1)} %get-tuple-element.140), channel_id=1, source_target_pairs={{1,0},{2,1},{3,2},{4,3},{5,4},{6,5},{7,6},{9,8},{10,9},{11,10},{12... | collective-permute-start | bytes 34568 | tf_op jit(solution)/shard_map/ppermute | solution.py:50
  71.5 19.4 %collective-permute-start.10 = (f32[3,10,3,32]{3,2,1,0:T(4,128)S(1)}, f32[3,10,3,32]{3,2,1,0:T(4,128)S(1)}, u32[]{:S(2)}, u32[]{:S(2)}) collective-permute-start(f32[3,10,3,32]{3,2,1,0:T(4,128)S(1)} %get-tuple-element.139), channel_id=1, source_target_pairs={{0,1},{1,2},{2,3},{3,4},{4,5},{5,6},{6,7},{8,9},{9,10},{10,11},{11... | collective-permute-start | bytes 34568 | tf_op jit(solution)/shard_map/ppermute | solution.py:47
  73.7 25.0 %collective-permute-start.7 = (f32[4,16,1,128]{3,2,1,0:T(1,128)S(1)}, f32[4,16,1,128]{3,2,1,0:T(1,128)S(1)}, u32[]{:S(2)}, u32[]{:S(2)}) collective-permute-start(f32[4,16,1,128]{3,2,1,0:T(1,128)S(1)} %get-tuple-element.115), channel_id=1, source_target_pairs={{1,0},{2,1},{3,2},{4,3},{5,4},{6,5},{7,6},{9,8},{10,9},{11,10},{12... | collective-permute-start | bytes 98312 | tf_op jit(solution)/shard_map/ppermute | solution.py:31
  82.2 16.5 %collective-permute-start.4 = (f32[4,16,1,128]{3,2,1,0:T(1,128)S(1)}, f32[4,16,1,128]{3,2,1,0:T(1,128)S(1)}, u32[]{:S(2)}, u32[]{:S(2)}) collective-permute-start(f32[4,16,1,128]{3,2,1,0:T(1,128)S(1)} %get-tuple-element.114), channel_id=1, source_target_pairs={{0,1},{1,2},{2,3},{3,4},{4,5},{5,6},{6,7},{8,9},{9,10},{10,11},{11... | collective-permute-start | bytes 98312 | tf_op jit(solution)/shard_map/ppermute | solution.py:30
  84.1 14.6 %collective-permute-start.6 = (f32[4,1,16,128]{3,2,1,0:T(8,128)S(1)}, f32[4,1,16,128]{3,2,1,0:T(8,128)S(1)}, u32[]{:S(2)}, u32[]{:S(2)}) collective-permute-start(f32[4,1,16,128]{3,2,1,0:T(8,128)S(1)} %get-tuple-element.113), channel_id=1, source_target_pairs={{8,0},{16,8},{24,16},{32,24},{40,32},{48,40},{56,48},{64,56},{72,6... | collective-permute-start | bytes 98312 | tf_op jit(solution)/shard_map/ppermute | solution.py:31
  88.8 10.0 %collective-permute-start.5 = (f32[4,1,16,128]{3,2,1,0:T(8,128)S(1)}, f32[4,1,16,128]{3,2,1,0:T(8,128)S(1)}, u32[]{:S(2)}, u32[]{:S(2)}) collective-permute-start(f32[4,1,16,128]{3,2,1,0:T(8,128)S(1)} %get-tuple-element.112), channel_id=1, source_target_pairs={{0,8},{8,16},{16,24},{24,32},{32,40},{40,48},{48,56},{56,64},{64,7... | collective-permute-start | bytes 98312 | tf_op jit(solution)/shard_map/ppermute | solution.py:30
  113.2 8.7 %collective-permute-start.17 = (f32[3,3,4,32]{3,2,1,0:T(4,128)S(1)}, f32[3,3,4,32]{3,2,1,0:T(4,128)S(1)}, u32[]{:S(2)}, u32[]{:S(2)}) collective-permute-start(f32[3,3,4,32]{3,2,1,0:T(4,128)S(1)} %get-tuple-element.144), channel_id=1, source_target_pairs={{8,0},{16,8},{24,16},{32,24},{40,32},{48,40},{56,48},{64,56},{72,6... | collective-permute-start | bytes 13832 | tf_op jit(solution)/shard_map/ppermute | solution.py:50
  119.5 7.9 %collective-permute-start.16 = (f32[3,3,4,32]{3,2,1,0:T(4,128)S(1)}, f32[3,3,4,32]{3,2,1,0:T(4,128)S(1)}, u32[]{:S(2)}, u32[]{:S(2)}) collective-permute-start(f32[3,3,4,32]{3,2,1,0:T(4,128)S(1)} %get-tuple-element.143), channel_id=1, source_target_pairs={{0,8},{8,16},{16,24},{24,32},{32,40},{40,48},{48,56},{56,64},{64,7... | collective-permute-start | bytes 13832 | tf_op jit(solution)/shard_map/ppermute | solution.py:47
  127.4 23.2 %collective-permute-start.19 = (f32[3,10,3,32]{3,2,1,0:T(4,128)S(1)}, f32[3,10,3,32]{3,2,1,0:T(4,128)S(1)}, u32[]{:S(2)}, u32[]{:S(2)}) collective-permute-start(f32[3,10,3,32]{3,2,1,0:T(4,128)S(1)} %get-tuple-element.138), channel_id=1, source_target_pairs={{1,0},{2,1},{3,2},{4,3},{5,4},{6,5},{7,6},{9,8},{10,9},{11,10},{12... | collective-permute-start | bytes 34568 | tf_op jit(solution)/shard_map/ppermute | solution.py:50
  136.1 17.2 %collective-permute-start.18 = (f32[3,10,3,32]{3,2,1,0:T(4,128)S(1)}, f32[3,10,3,32]{3,2,1,0:T(4,128)S(1)}, u32[]{:S(2)}, u32[]{:S(2)}) collective-permute-start(f32[3,10,3,32]{3,2,1,0:T(4,128)S(1)} %get-tuple-element.137), channel_id=1, source_target_pairs={{0,1},{1,2},{2,3},{3,4},{4,5},{5,6},{6,7},{8,9},{9,10},{10,11},{11... | collective-permute-start | bytes 34568 | tf_op jit(solution)/shard_map/ppermute | solution.py:47
  138.0 23.1 %collective-permute-start.15 = (f32[4,16,1,128]{3,2,1,0:T(1,128)S(1)}, f32[4,16,1,128]{3,2,1,0:T(1,128)S(1)}, u32[]{:S(2)}, u32[]{:S(2)}) collective-permute-start(f32[4,16,1,128]{3,2,1,0:T(1,128)S(1)} %get-tuple-element.111), channel_id=1, source_target_pairs={{1,0},{2,1},{3,2},{4,3},{5,4},{6,5},{7,6},{9,8},{10,9},{11,10},{12... | collective-permute-start | bytes 98312 | tf_op jit(solution)/shard_map/ppermute | solution.py:31
  146.8 14.4 %collective-permute-start.12 = (f32[4,16,1,128]{3,2,1,0:T(1,128)S(1)}, f32[4,16,1,128]{3,2,1,0:T(1,128)S(1)}, u32[]{:S(2)}, u32[]{:S(2)}) collective-permute-start(f32[4,16,1,128]{3,2,1,0:T(1,128)S(1)} %get-tuple-element.110), channel_id=1, source_target_pairs={{0,1},{1,2},{2,3},{3,4},{4,5},{5,6},{6,7},{8,9},{9,10},{10,11},{11... | collective-permute-start | bytes 98312 | tf_op jit(solution)/shard_map/ppermute | solution.py:30
  148.7 12.4 %collective-permute-start.14 = (f32[4,1,16,128]{3,2,1,0:T(8,128)S(1)}, f32[4,1,16,128]{3,2,1,0:T(8,128)S(1)}, u32[]{:S(2)}, u32[]{:S(2)}) collective-permute-start(f32[4,1,16,128]{3,2,1,0:T(8,128)S(1)} %get-tuple-element.109), channel_id=1, source_target_pairs={{8,0},{16,8},{24,16},{32,24},{40,32},{48,40},{56,48},{64,56},{72,6... | collective-permute-start | bytes 98312 | tf_op jit(solution)/shard_map/ppermute | solution.py:31
  150.6 10.5 %collective-permute-start.13 = (f32[4,1,16,128]{3,2,1,0:T(8,128)S(1)}, f32[4,1,16,128]{3,2,1,0:T(8,128)S(1)}, u32[]{:S(2)}, u32[]{:S(2)}) collective-permute-start(f32[4,1,16,128]{3,2,1,0:T(8,128)S(1)} %get-tuple-element.108), channel_id=1, source_target_pairs={{0,8},{8,16},{16,24},{24,32},{32,40},{40,48},{48,56},{56,64},{64,7... | collective-permute-start | bytes 98312 | tf_op jit(solution)/shard_map/ppermute | solution.py:30
  172.8 12.6 %collective-permute-start.21 = (f32[3,3,4,32]{3,2,1,0:T(4,128)S(1)}, f32[3,3,4,32]{3,2,1,0:T(4,128)S(1)}, u32[]{:S(2)}, u32[]{:S(2)}) collective-permute-start(f32[3,3,4,32]{3,2,1,0:T(4,128)S(1)} %get-tuple-element.142), channel_id=1, source_target_pairs={{8,0},{16,8},{24,16},{32,24},{40,32},{48,40},{56,48},{64,56},{72,6... | collective-permute-start | bytes 13832 | tf_op jit(solution)/shard_map/ppermute | solution.py:50
  178.7 7.8 %collective-permute-start.20 = (f32[3,3,4,32]{3,2,1,0:T(4,128)S(1)}, f32[3,3,4,32]{3,2,1,0:T(4,128)S(1)}, u32[]{:S(2)}, u32[]{:S(2)}) collective-permute-start(f32[3,3,4,32]{3,2,1,0:T(4,128)S(1)} %get-tuple-element.141), channel_id=1, source_target_pairs={{0,8},{8,16},{16,24},{24,32},{32,40},{40,48},{48,56},{56,64},{64,7... | collective-permute-start | bytes 13832 | tf_op jit(solution)/shard_map/ppermute | solution.py:47
  186.5 11.4 %collective-permute-start.23 = (f32[3,10,3,32]{3,2,1,0:T(4,128)S(1)}, f32[3,10,3,32]{3,2,1,0:T(4,128)S(1)}, u32[]{:S(2)}, u32[]{:S(2)}) collective-permute-start(f32[3,10,3,32]{3,2,1,0:T(4,128)S(1)} %get-tuple-element.136), channel_id=1, source_target_pairs={{1,0},{2,1},{3,2},{4,3},{5,4},{6,5},{7,6},{9,8},{10,9},{11,10},{12... | collective-permute-start | bytes 34568 | tf_op jit(solution)/shard_map/ppermute | solution.py:50
  195.3 10.9 %collective-permute-start.22 = (f32[3,10,3,32]{3,2,1,0:T(4,128)S(1)}, f32[3,10,3,32]{3,2,1,0:T(4,128)S(1)}, u32[]{:S(2)}, u32[]{:S(2)}) collective-permute-start(f32[3,10,3,32]{3,2,1,0:T(4,128)S(1)} %get-tuple-element.135), channel_id=1, source_target_pairs={{0,1},{1,2},{2,3},{3,4},{4,5},{5,6},{6,7},{8,9},{9,10},{10,11},{11... | collective-permute-start | bytes 34568 | tf_op jit(solution)/shard_map/ppermute | solution.py:47
where the time goes:
time: 208 us; the launch traced here: 207 us
  starting transfers between devices  105 us (50%)
  local copies, waits for them, and re-layouts  49.7 us (24%)
  other arithmetic  36 us (17%)
  waiting for transfers between devices  15.7 us (8%)
    ppermute x6, starting transfers between devices, extended(): lax.ppermute(lax.slice_in_dim(block, 0, width, axis=dim), axis, backward)  43.5 us
    ppermute x6, starting transfers between devices, padded(): lax.ppermute(first, axis, [(b, a) for a, b in up])  36.9 us
    reshape x3, local copies, waits for them, and re-layouts, restrict(): fine.reshape(lattice_span[0] // COARSEN_RATIO, COARSEN_RATIO, lattice_spa...  17.8 us
    ppermute x6, waiting for transfers between devices, extended(): lax.ppermute(lax.slice_in_dim(block, block.shape[dim] - width, None, axis...  15.7 us
    div x3, local copies, waits for them, and re-layouts, per_device(): 1.0 / (1.0 + speed_falloff * refine_warmth(pointwise_warmth))  14.6 us
    another operation x7, other arithmetic, linearized_correction(): return (jnp.stack([new_pot, new_elec, new_hole], 0), warming_field)  14.2 us
    ppermute x6, starting transfers between devices, padded(): lax.ppermute(last, axis, up)  12.4 us
    ppermute x6, starting transfers between devices, extended(): lax.ppermute(lax.slice_in_dim(block, block.shape[dim] - width, None, axis...  11.8 us
  transfers between devices with their start and end apart: 24, of which 4 were waited for; matrix products, arithmetic and copies ran while one was open for 22% of the time, Pallas kernels for 0%

commit v1 on v0

v1 whole, which is shorter than its diff:
```python
import functools

import jax
import jax.numpy as jnp
from jax import lax
from jax.experimental import pallas as pl
from jax.experimental.pallas import tpu as pltpu
from jax.sharding import PartitionSpec as P

NEWTON = 3
SWEEPS = 3
SIDE = 16
LANES = 128
CELLS = 4
NODES = SIDE * SIDE

CHARGE = 4.0
SHIFT = 24.0
BIAS = 0.25
HEAT_GAIN = 1.0
SINK = 0.3
DROP = 0.5

F32 = jnp.float32
MESH = pl.DeviceIdType.MESH
OPPOSITE = (1, 0, 3, 2)
DIAGONAL_OPPOSITE = (3, 2, 1, 0)


def face(pi, ni, qi, pj, nj, qj):
    d = pj - pi
    u = jnp.abs(d)
    v = d * d
    small = u < 0.5
    r = 1.0 / (jnp.exp(u) - 1.0)
    wide = u * r
    g_near = 1.0 + v * (1.0 / 12.0 + v * (-1.0 / 720.0 + v * (1.0 / 30240.0 + v * (-1.0 / 1209600.0))))
    h_near = u * (1.0 / 6.0 + v * (-1.0 / 180.0 + v * (1.0 / 5040.0 + v * (-1.0 / 151200.0))))
    b = jnp.where(small, g_near - 0.5 * u, wide)
    h = jnp.where(small, h_near, r * (1.0 - wide) - wide + 0.5)
    g = b + 0.5 * u
    h = jnp.where(d < 0.0, -h, h)
    plus = b + jnp.maximum(-d, 0.0)
    minus = b + jnp.maximum(d, 0.0)
    je = nj * plus - ni * minus
    jh = qj * minus - qi * plus
    gn = 0.5 * (nj + ni) - h * (nj - ni)
    gp = -0.5 * (qj + qi) - h * (qj - qi)
    return d, je, jh, gn, gp, g


def spread(a, lane):
    a = a + jnp.where((lane & 1) == 0, pltpu.roll(a, LANES - 1, 1), pltpu.roll(a, 1, 1))
    return a + jnp.where((lane & 2) == 0, pltpu.roll(a, LANES - 2, 1), pltpu.roll(a, 2, 1))


def body(
    nx, ny,
    sol_ref, ins_ref, ele_ref, imp_ref, con_ref, war_ref,
    out_ref, temp_ref,
    st, eps, ins, ele, wl, fc, acc, hs, yq, mob, dop, rep, small, wbx, wby,
    hx, hy, hex_, se, sy, ts, ds, tr, dr, tx, sx, cx, ix, dd,
    load_sem, store_sem, s_send, s_recv, e_send, e_recv, t_send, t_recv, d_send, d_recv,
):
    gx = lax.axis_index("gx")
    gy = lax.axis_index("gy")
    xl, xh = lax.rem(gx + nx - 1, nx), lax.rem(gx + 1, nx)
    yl, yh = lax.rem(gy + ny - 1, ny), lax.rem(gy + 1, ny)
    near = ((xl, gy), (xh, gy), (gx, yl), (gx, yh))
    corner = ((xl, yl), (xl, yh), (xh, yl), (xh, yh))
    has = (gx > 0, gx < nx - 1, gy > 0, gy < ny - 1)
    has_corner = (has[0] & has[2], has[0] & has[3], has[1] & has[2], has[1] & has[3])

    barrier = pltpu.get_barrier_semaphore()
    for target in near + corner:
        pl.semaphore_signal(barrier, inc=1, device_id=target, device_id_type=MESH)

    loads = [
        pltpu.make_async_copy(sol_ref, st, load_sem.at[0]),
        pltpu.make_async_copy(ins_ref, ins, load_sem.at[1]),
        pltpu.make_async_copy(ele_ref, ele, load_sem.at[2]),
    ]
    for copy in loads:
        copy.start()

    lane = lax.broadcasted_iota(jnp.int32, (1, LANES), 1)
    lane4 = lane & 3
    last_lane = (lane != LANES - 1).astype(F32)
    last_row = (lax.broadcasted_iota(jnp.int32, (SIDE, LANES), 0) != SIDE - 1).astype(F32)

    def slab(x):
        return pl.ds(pl.multiple_of(x * SIDE, SIDE), SIDE)

    def remote(src, dst, send, recv, target):
        return pltpu.make_async_remote_copy(
            src_ref=src, dst_ref=dst, send_sem=send, recv_sem=recv, device_id=target, device_id_type=MESH
        )

    def state_copies(k):
        out = []
        for s in range(4):
            if s < 2:
                src = st.at[:, pl.ds(0 if s == 0 else NODES - SIDE, SIDE), :]
                dst = hx.at[k, OPPOSITE[s]]
            else:
                src, dst = sy.at[s - 2], hy.at[k, OPPOSITE[s] - 2]
            out.append(remote(src, dst, s_send.at[k, s], s_recv.at[k, OPPOSITE[s]], near[s]))
        return out

    def eps_copies():
        out = []
        for s in range(4):
            src = eps.at[pl.ds(0 if s == 0 else NODES - SIDE, SIDE), :] if s < 2 else se.at[s - 2]
            out.append(remote(src, hex_.at[OPPOSITE[s]], e_send.at[s], e_recv.at[OPPOSITE[s]], near[s]))
        return out

    def thermal_copies(t):
        out = []
        for s in range(4):
            o = OPPOSITE[s]
            out.append(remote(ts.at[t], tr.at[t, o], t_send.at[t, s], t_recv.at[t, o], near[s]))
        for s in range(4):
            o = DIAGONAL_OPPOSITE[s]
            out.append(remote(ds.at[t, s], dr.at[t, o], d_send.at[t, s], d_recv.at[t, o], corner[s]))
        return out

    def pack_rows():
        for f in range(3):
            sy[0, f] = st[f, pl.ds(0, SIDE, stride=SIDE), :]
            sy[1, f] = st[f, pl.ds(SIDE - 1, SIDE, stride=SIDE), :]

    def pack_thermal(t, warm, source):
        ts[t, 0:4, :] = warm
        ts[t, 4:8, :] = source
        tile = ts[t]
        up2, down2 = pltpu.roll(tile, 2, 1), pltpu.roll(tile, LANES - 2, 1)
        up3, down3 = pltpu.roll(tile, 3, 1), pltpu.roll(tile, LANES - 3, 1)

        def low(a, b):
            return jnp.where(lane4 < 2, tile[a:a + 1], jnp.where(lane4 == 2, up2[b:b + 1], up3[a + 4:a + 5]))

        def high(a, b):
            return jnp.where(lane4 >= 2, tile[a:a + 1], jnp.where(lane4 == 1, down2[b:b + 1], down3[a + 4:a + 5]))

        ds[t, 0] = low(0, 1)
        ds[t, 1] = high(0, 1)
        ds[t, 2] = low(3, 2)
        ds[t, 3] = high(3, 2)

    def keep(flag, a):
        return jnp.where(flag, a, jnp.zeros_like(a))

    def load_corners(t):
        for s in range(4):
            dd[s:s + 1, :] = keep(has_corner[s], dr[t, s])

    def gather_source(t, into):
        tile = dd[...]
        up3, down3 = pltpu.roll(tile, 3, 1), pltpu.roll(tile, LANES - 3, 1)
        into[1, 0:2, :] = keep(has[0], tr[t, 0, 6:8, :])
        into[1, 2:6, :] = ts[t, 4:8, :]
        into[1, 6:8, :] = keep(has[1], tr[t, 1, 4:6, :])
        into[0, 2:6, :] = keep(has[2], tr[t, 2, 4:8, :])
        into[2, 2:6, :] = keep(has[3], tr[t, 3, 4:8, :])
        into[0, 1:2, :] = up3[0:1]
        into[0, 6:7, :] = up3[2:3]
        into[2, 1:2, :] = down3[1:2]
        into[2, 6:7, :] = down3[3:4]

    def gather_warm(t):
        tile = dd[...]
        up2, down2 = pltpu.roll(tile, 2, 1), pltpu.roll(tile, LANES - 2, 1)
        tx[1, 0:3, :] = keep(has[0], tr[t, 0, 1:4, :])
        tx[1, 3:7, :] = ts[t, 0:4, :]
        tx[1, 7:10, :] = keep(has[1], tr[t, 1, 0:3, :])
        tx[0, 3:7, :] = keep(has[2], tr[t, 2, 0:4, :])
        tx[2, 3:7, :] = keep(has[3], tr[t, 3, 0:4, :])
        tx[0, 1:2, :] = up2[0:1]
        tx[0, 2:3, :] = tile[0:1]
        tx[0, 7:8, :] = tile[2:3]
        tx[0, 8:9, :] = up2[2:3]
        tx[2, 1:2, :] = down2[1:2]
        tx[2, 2:3, :] = tile[1:2]
        tx[2, 7:8, :] = tile[3:4]
        tx[2, 8:9, :] = down2[3:4]

    def relax(t):
        load_corners(t)
        gather_source(t, sx)
        gather_warm(t)
        for _ in range(SWEEPS):
            mid = [tx[b, 1:9, :] for b in range(3)]
            new = []
            for b in range(3):
                c = mid[b]
                z_low = jnp.where(lane >= 4, pltpu.roll(c, 4, 1), 0.0)
                z_high = jnp.where(lane < LANES - 4, pltpu.roll(c, LANES - 4, 1), 0.0)
                y_low, y_high = pltpu.roll(c, 1, 1), pltpu.roll(c, LANES - 1, 1)
                if b > 0:
                    y_low = jnp.where(lane4 > 0, y_low, pltpu.roll(mid[b - 1], LANES - 3, 1))
                if b < 2:
                    y_high = jnp.where(lane4 < 3, y_high, pltpu.roll(mid[b + 1], 3, 1))
                total = (tx[b, 0:8, :] + tx[b, 2:10, :]) + (y_low + y_high) + (z_low + z_high)
                new.append((sx[b] + cx[b] * total) * ix[b])
            for b in range(3):
                tx[b, 1:9, :] = new[b]
        return tx[1, 3:7, :]

    def lookup(labels, table):
        result = jnp.zeros(labels.shape, F32)
        for level, amount in enumerate(table):
            result = jnp.where(labels == level, amount, result)
        return result

    for c in range(CELLS):
        small[4 * c:4 * c + 4, :] = lookup(imp_ref[c], (-2.0, -0.5, 0.5, 2.0))
        small[16 + 4 * c:16 + 4 * c + 4, :] = lookup(con_ref[c], (0.5, 1.0, 2.0, 4.0))
        small[32 + 4 * c:32 + 4 * c + 4, :] = war_ref[c]
    zc = LANES // 4
    wide = (lax.broadcasted_iota(jnp.int32, (zc, LANES), 1) // 4 == lax.broadcasted_iota(jnp.int32, (zc, LANES), 0)).astype(F32)
    rep[...] = jnp.dot(small[...], wide, precision=lax.Precision.HIGHEST, preferred_element_type=F32)
    for c in range(CELLS):
        for y in range(CELLS):
            dop[c, 4 * y:4 * y + 4, :] = jnp.broadcast_to(rep[4 * c + y:4 * c + y + 1, :], (4, LANES))

    def packed(first):
        rows = [rep[pl.ds(first + y, 4, stride=4), :] for y in range(CELLS)]
        return jnp.where(lane4 == 0, rows[0], jnp.where(lane4 == 1, rows[1], jnp.where(lane4 == 2, rows[2], rows[3])))

    cond, warm0 = packed(16), packed(32)
    pack_thermal(0, cond, cond)
    ts[1, 0:4, :] = warm0
    tx[...] = jnp.zeros_like(tx)
    sx[...] = jnp.zeros_like(sx)
    cx[...] = jnp.zeros_like(cx)
    dd[...] = jnp.zeros_like(dd)

    for copy in loads:
        copy.wait()
    pack_rows()
    eps[...] = jnp.where(ins[...] == 1, 0.4, 1.0).astype(F32)
    se[0] = eps[pl.ds(0, SIDE, stride=SIDE), :]
    se[1] = eps[pl.ds(SIDE - 1, SIDE, stride=SIDE), :]

    pl.semaphore_wait(barrier, 8)
    for copy in state_copies(0) + eps_copies() + thermal_copies(0):
        copy.start()

    def weigh(x, below, upper):
        e = eps[slab(x), :]
        wy = (e + pltpu.roll(e, SIDE - 1, 0)) * last_row
        wz = (e + pltpu.roll(e, LANES - 1, 1)) * last_lane
        wl[1, slab(x), :] = wy
        wl[2, slab(x), :] = wz
        total = below + wy + pltpu.roll(wy, 1, 0) + wz + pltpu.roll(wz, 1, 1)
        if not upper:
            fc[slab(x), :] = total
            return below
        wx = e + eps[slab(x + 1), :]
        wl[0, slab(x), :] = wx
        fc[slab(x), :] = total + wx
        return wx

    zero = jnp.zeros((SIDE, LANES), F32)
    below = lax.fori_loop(0, SIDE - 1, lambda x, b: weigh(x, b, True), zero)
    weigh(SIDE - 1, below, False)

    def fluxes(x, below, upper):
        psi, n, p = (st[f, slab(x), :] for f in range(3))
        d, je, jh, gn, gp, g = face(psi, n, p, *(pltpu.roll(a, SIDE - 1, 0) for a in (psi, n, p)))
        je, jh, gn, gp, g, ld = (a * last_row for a in (je, jh, gn, gp, g, d))
        lap = wl[1, slab(x), :] * d
        t = je - jh
        sums = [je, jh, lap, ld, gn, gp, g, t * t]
        sums = [a - pltpu.roll(a, 1, 0) if i < 4 else a + pltpu.roll(a, 1, 0) for i, a in enumerate(sums)]
        d, je, jh, gn, gp, g = face(psi, n, p, *(pltpu.roll(a, LANES - 1, 1) for a in (psi, n, p)))
        je, jh, gn, gp, g, ld = (a * last_lane for a in (je, jh, gn, gp, g, d))
        lap = wl[2, slab(x), :] * d
        t = je - jh
        more = [je, jh, lap, ld, gn, gp, g, t * t]
        more = [a - pltpu.roll(a, 1, 1) if i < 4 else a + pltpu.roll(a, 1, 1) for i, a in enumerate(more)]
        sums = [a + b for a, b in zip(sums, more)]
        sums = [a - b if i < 4 else a + b for i, (a, b) in enumerate(zip(sums, below))]
        carry = below
        if upper:
            d, je, jh, gn, gp, g = face(psi, n, p, *(st[f, slab(x + 1), :] for f in range(3)))
            t = je - jh
            carry = (je, jh, wl[0, slab(x), :] * d, d, gn, gp, g, t * t)
            sums = [a + b for a, b in zip(sums, carry)]
        for q in range(7):
            acc[q, slab(x), :] = sums[q]
        cell = slab(x // CELLS)
        hs[cell, :] = hs[cell, :] + sums[7] / (n + p)
        return carry

    def edge(side, mine, halo, weight):
        scale = has[side].astype(F32)
        if side % 2 == 0:
            d, je, jh, gn, gp, g = face(*halo, *mine)
            sign = -scale
        else:
            d, je, jh, gn, gp, g = face(*mine, *halo)
            sign = scale
        t = (je - jh) * scale
        return (je * sign, jh * sign, weight * d * sign, d * sign, gn * scale, gp * scale, g * scale), t * t

    def step(k, nothing):
        hs[...] = jnp.zeros_like(hs)
        none = (zero,) * 8
        below = lax.fori_loop(0, SIDE - 1, lambda x, b: fluxes(x, b, True), none)
        fluxes(SIDE - 1, below, False)

        @pl.when(k == 0)
        def _():
            for copy in eps_copies() + thermal_copies(0):
                copy.wait()
            for s in range(2):
                rows = pl.ds(s * (NODES - SIDE), SIDE)
                wbx[s] = eps[rows, :] + hex_[s]
                fc[rows, :] = fc[rows, :] + wbx[s] * has[s].astype(F32)
            for s in range(2):
                rows = pl.ds(s * (SIDE - 1), SIDE, stride=SIDE)
                wby[s] = se[s] + hex_[2 + s]
                fc[rows, :] = fc[rows, :] + wby[s] * has[2 + s].astype(F32)
            load_corners(0)
            gather_source(0, cx)
            ix[...] = 1.0 / (SINK + 6.0 * cx[...])

        @pl.when(k > 0)
        def _():
            for copy in thermal_copies(k):
                copy.wait()
            ts[k + 1, 0:4, :] = relax(k)

        warm = ts[k + 1, 0:4, :]
        m = 1.0 / (1.0 + DROP * warm)
        m4 = spread(jnp.concatenate([jnp.where(lane4 == y, m, 0.0) for y in range(CELLS)], 0), lane)
        rep[0:16, :] = m4
        for c in range(CELLS):
            for y in range(CELLS):
                mob[c, 4 * y:4 * y + 4, :] = jnp.broadcast_to(rep[4 * y + c:4 * y + c + 1, :], (4, LANES))

        for copy in state_copies(k):
            copy.wait()
        for s in range(2):
            rows = pl.ds(s * (NODES - SIDE), SIDE)
            mine = [st[f, rows, :] for f in range(3)]
            sums, heat = edge(s, mine, [hx[k, s, f] for f in range(3)], wbx[s])
            for q in range(7):
                acc[q, rows, :] = acc[q, rows, :] + sums[q]
            cell = pl.ds(s * (64 - SIDE), SIDE)
            hs[cell, :] = hs[cell, :] + heat / (mine[1] + mine[2])
        for s in range(2):
            rows = pl.ds(s * (SIDE - 1), SIDE, stride=SIDE)
            mine = [sy[s, f] for f in range(3)]
            sums, heat = edge(2 + s, mine, [hy[k, s, f] for f in range(3)], wby[s])
            for q in range(7):
                acc[q, rows, :] = acc[q, rows, :] + sums[q]
            yq[s] = heat / (mine[1] + mine[2])

        parts = []
        for y in range(CELLS):
            total = hs[pl.ds(4 * y, 4, stride=SIDE), :]
            for i in range(1, 4):
                total = total + hs[pl.ds(4 * y + i, 4, stride=SIDE), :]
            if y in (0, CELLS - 1):
                for i in range(4):
                    total = total + yq[y // (CELLS - 1), pl.ds(i, 4, stride=4), :]
            parts.append(total)
        rep[0:16, :] = spread(jnp.concatenate(parts, 0), lane)
        r = [rep[4 * y:4 * y + 4, :] for y in range(CELLS)]
        heat = jnp.where(lane4 == 0, r[0], jnp.where(lane4 == 1, r[1], jnp.where(lane4 == 2, r[2], r[3])))
        pack_thermal(k + 1, warm, heat * m * (HEAT_GAIN * 0.5 / 64.0))
        for copy in thermal_copies(k + 1):
            copy.start()

        def solve(x, nothing):
            rows = slab(x)
            psi, n, p = (st[f, rows, :] for f in range(3))
            fe, fh, lap, ls, gn, gp, gs = (acc[q, rows, :] for q in range(7))
            cell = x // CELLS
            mu, level = mob[cell], dop[cell]
            contact = ele[rows, :] == 1
            rd = 1.0 / (n + p + 2.0)
            rec = (n * p - 1.0) * rd
            rn, rp = (p + 1.0) * rd, (n + 1.0) * rd
            rn, rp = rn * rn, rp * rp
            r0 = lap + CHARGE * (p - n + level)
            r1 = mu * fe - rec
            r2 = mu * fh - rec
            aa = -fc[rows, :]
            ba, ca = mu * gn, mu * gp
            bb = -mu * (gs + 0.5 * ls) - rn - SHIFT
            cc = -mu * (gs - 0.5 * ls) - rp - SHIFT
            bc, cb = -rp, -rn
            c_aa = bb * cc - bc * cb
            c_ab = bc * ca - ba * cc
            c_ac = ba * cb - bb * ca
            inv = 1.0 / (aa * c_aa + CHARGE * (c_ac - c_ab))
            d0 = (c_aa * r0 + CHARGE * ((cb + cc) * r1 - (bc + bb) * r2)) * inv
            d1 = (c_ab * r0 + (aa * cc - CHARGE * ca) * r1 + (CHARGE * ba - aa * bc) * r2) * inv
            d2 = (c_ac * r0 - (CHARGE * ca + aa * cb) * r1 + (aa * bb + CHARGE * ba) * r2) * inv
            d0 = jnp.where(contact, psi - BIAS * level, d0)
            d1 = jnp.where(contact, n - 1.0, d1)
            d2 = jnp.where(contact, p - 1.0, d2)
            st[0, rows, :] = psi - d0
            st[1, rows, :] = n * jnp.exp(-d1 / n)
            st[2, rows, :] = p * jnp.exp(-d2 / p)
            return nothing

        lax.fori_loop(0, SIDE, solve, 0)

        @pl.when(k < NEWTON - 1)
        def _():
            pack_rows()
            for copy in state_copies(k + 1):
                copy.start()

        return nothing

    lax.fori_loop(0, NEWTON, step, 0)

    store = pltpu.make_async_copy(st, out_ref, store_sem)
    store.start()
    for copy in thermal_copies(NEWTON):
        copy.wait()
    warm = relax(NEWTON)
    cells = jnp.concatenate([jnp.where(lane4 == y, warm, 0.0) for y in range(CELLS)], 0)
    narrow = (lax.broadcasted_iota(jnp.int32, (LANES, zc), 0) // 4 == lax.broadcasted_iota(jnp.int32, (LANES, zc), 1)).astype(F32)
    cells = jnp.dot(cells, narrow, precision=lax.Precision.HIGHEST, preferred_element_type=F32)
    for c in range(CELLS):
        for y in range(CELLS):
            temp_ref[c, y:y + 1, :] = cells[4 * y + c:4 * y + c + 1, :]
    store.wait()


def solution(mesh):
    nx, ny = mesh.shape["gx"], mesh.shape["gy"]

    def per_device(sol, ins, ele, imp, con, war):
        vm = pltpu.VMEM
        dma = pltpu.SemaphoreType.DMA
        tile = (SIDE, LANES)
        call = pl.pallas_call(
            functools.partial(body, nx, ny),
            out_shape=(
                jax.ShapeDtypeStruct((3, NODES, LANES), F32),
                jax.ShapeDtypeStruct((CELLS, CELLS, LANES // 4), F32),
            ),
            in_specs=[pl.BlockSpec(memory_space=pl.ANY)] * 3 + [pl.BlockSpec(memory_space=pltpu.VMEM)] * 3,
            out_specs=(pl.BlockSpec(memory_space=pl.ANY), pl.BlockSpec(memory_space=pltpu.VMEM)),
            scratch_shapes=[
                vm((3, NODES, LANES), F32),
                vm((NODES, LANES), F32),
                vm((NODES, LANES), jnp.int32),
                vm((NODES, LANES), jnp.int32),
                vm((3, NODES, LANES), F32),
                vm((NODES, LANES), F32),
                vm((7, NODES, LANES), F32),
                vm((64, LANES), F32),
                vm((2,) + tile, F32),
                vm((CELLS,) + tile, F32),
                vm((CELLS,) + tile, F32),
                vm((48, LANES), F32),
                vm((48, LANES // 4), F32),
                vm((2,) + tile, F32),
                vm((2,) + tile, F32),
                vm((NEWTON, 2, 3) + tile, F32),
                vm((NEWTON, 2, 3) + tile, F32),
                vm((4,) + tile, F32),
                vm((2,) + tile, F32),
                vm((2, 3) + tile, F32),
                vm((NEWTON + 1, 8, LANES), F32),
                vm((NEWTON + 1, 4, 1, LANES), F32),
                vm((NEWTON + 1, 4, 8, LANES), F32),
                vm((NEWTON + 1, 4, 1, LANES), F32),
                vm((3, SIDE, LANES), F32),
                vm((3, 8, LANES), F32),
                vm((3, 8, LANES), F32),
                vm((3, 8, LANES), F32),
                vm((8, LANES), F32),
                dma((3,)),
                dma,
                dma((NEWTON, 4)),
                dma((NEWTON, 4)),
                dma((4,)),
                dma((4,)),
                dma((NEWTON + 1, 4)),
                dma((NEWTON + 1, 4)),
                dma((NEWTON + 1, 4)),
                dma((NEWTON + 1, 4)),
            ],
            compiler_params=pltpu.CompilerParams(collective_id=0, has_side_effects=True),
        )
        state, warm = call(
            sol.reshape(3, NODES, LANES), ins.reshape(NODES, LANES), ele.reshape(NODES, LANES), imp, con, war
        )
        return state.reshape(3, SIDE, SIDE, LANES), warm

    spec = P("gx", "gy", None)
    return jax.shard_map(
        per_device,
        mesh=mesh,
        in_specs=(P(None, "gx", "gy", None),) + (spec,) * 5,
        out_specs=(P(None, "gx", "gy", None), spec),
        check_vma=False,
    )
```

time: 208 us -> 47.4 us (0.23)
  the two profiles are of different devices: /device:TPU:14 before, /device:TPU:9 now
where the time goes in v1:
time: 47.4 us; the launch traced here: 47.2 us
  Pallas kernels  44.2 us (93%)
  local copies, waits for them, and re-layouts  2.37 us (5%)
  between operations  0.65 us (1%)
    pallas_call x1, Pallas kernels, per_device(): call(sol.reshape(3, NODES, LANES), ins.reshape(NODES, LANES), ele.reshape...  44.2 us
    unnamed x4, local copies, waits for them, and re-layouts  2.37 us

profile of v1, /device:TPU:9, one launch (start us, length us, event | category | flops | bytes accessed | tf_op | source)
XLA Modules:
  0.0 47.2 jit_solution(10024126265402169616)
XLA Ops:
  0.6 44.2 %shard_map.77 = (f32[3,256,128]{2,1,0:T(8,128)}, f32[4,4,32]{2,1,0:T(4,128)}) custom-call(f32[3,256,128]{2,1,0:T(8,128)} %bitcast.5, s32[256,128]{1,0:T(8,128)} %bitcast.6, s32[256,128]{1,0:T(8,128)} %bitcast.7, s32[4,4,32]{2,1,0:T(4,128)} %imp_ref.1, s32[4,4,32]{2,1,0:T(4,128)} %con_ref.1, f32[4,4,32]{2,1,0:T(4,128)} %war_ref.1), custom_call_target="tpu_custom_call" | custom-call | tf_op jit(solution)/shard_map/pallas_call | solution.py:495
  44.8 0.0 copy-start
  44.8 1.8 %copy.10 = f32[3,16,16,128]{3,2,1,0:T(8,128)} copy(f32[3,16,16,128]{3,2,1,0:T(8,128)} %bitcast.4) | data formatting | bytes 786432
  46.6 0.0 copy-done
  46.6 0.6 %copy.11 = f32[4,4,32]{2,1,0:T(4,128)} copy(f32[4,4,32]{2,1,0:T(4,128)S(1)} %copy-done) | data formatting | bytes 4096
Async XLA Ops:
  44.8 1.8 %copy-start = (f32[4,4,32]{2,1,0:T(4,128)S(1)}, f32[4,4,32]{2,1,0:T(4,128)}, u32[]{:S(2)}) copy-start(f32[4,4,32]{2,1,0:T(4,128)} %get-tuple-element.9) | copy-start | bytes 6148

commit v2 on v1

--- a/solution.py
+++ b/solution.py
@@ -58,7 +58,7 @@
     nx, ny,
     sol_ref, ins_ref, ele_ref, imp_ref, con_ref, war_ref,
     out_ref, temp_ref,
-    st, eps, ins, ele, wl, fc, acc, hs, yq, mob, dop, rep, small, wbx, wby,
+    st, eps, ins, ele, imp, con, war, wl, fc, acc, hs, yq, mob, dop, moby, dopy, rep, small, wbx, wby,
     hx, hy, hex_, se, sy, ts, ds, tr, dr, tx, sx, cx, ix, dd,
     load_sem, store_sem, s_send, s_recv, e_send, e_recv, t_send, t_recv, d_send, d_recv,
 ):
@@ -72,13 +72,19 @@
     has_corner = (has[0] & has[2], has[0] & has[3], has[1] & has[2], has[1] & has[3])
 
     barrier = pltpu.get_barrier_semaphore()
-    for target in near + corner:
-        pl.semaphore_signal(barrier, inc=1, device_id=target, device_id_type=MESH)
+    for s in (2, 3, 0, 1):
+
+        @pl.when(has[s])
+        def _():
+            pl.semaphore_signal(barrier, inc=1, device_id=near[s], device_id_type=MESH)
 
     loads = [
         pltpu.make_async_copy(sol_ref, st, load_sem.at[0]),
         pltpu.make_async_copy(ins_ref, ins, load_sem.at[1]),
-        pltpu.make_async_copy(ele_ref, ele, load_sem.at[2]),
+        pltpu.make_async_copy(imp_ref, imp, load_sem.at[2]),
+        pltpu.make_async_copy(con_ref, con, load_sem.at[3]),
+        pltpu.make_async_copy(war_ref, war, load_sem.at[4]),
+        pltpu.make_async_copy(ele_ref, ele, load_sem.at[5]),
     ]
     for copy in loads:
         copy.start()
@@ -95,6 +101,27 @@
         return pltpu.make_async_remote_copy(
             src_ref=src, dst_ref=dst, send_sem=send, recv_sem=recv, device_id=target, device_id_type=MESH
         )
+
+    def start(copies, flags, order):
+        for s in order:
+
+            @pl.when(flags[s])
+            def _():
+                copies[s].start()
+
+    def wait_sent(copies, flags):
+        for s in range(4):
+
+            @pl.when(flags[s])
+            def _():
+                copies[s].wait_send()
+
+    def wait_arrived(copies, flags, opposite):
+        for s in range(4):
+
+            @pl.when(flags[s])
+            def _():
+                copies[opposite[s]].wait_recv()
 
     def state_copies(k):
         out = []
@@ -115,14 +142,26 @@
         return out
 
     def thermal_copies(t):
-        out = []
+        sides, corners = [], []
         for s in range(4):
             o = OPPOSITE[s]
-            out.append(remote(ts.at[t], tr.at[t, o], t_send.at[t, s], t_recv.at[t, o], near[s]))
+            sides.append(remote(ts.at[t], tr.at[t, o], t_send.at[t, s], t_recv.at[t, o], near[s]))
         for s in range(4):
             o = DIAGONAL_OPPOSITE[s]
-            out.append(remote(ds.at[t, s], dr.at[t, o], d_send.at[t, s], d_recv.at[t, o], corner[s]))
-        return out
+            corners.append(remote(ds.at[t, s], dr.at[t, o], d_send.at[t, s], d_recv.at[t, o], corner[s]))
+        return sides, corners
+
+    def start_thermal(t):
+        sides, corners = thermal_copies(t)
+        start(corners, has_corner, range(4))
+        start(sides, has, (2, 3, 0, 1))
+
+    def wait_thermal(t):
+        sides, corners = thermal_copies(t)
+        wait_arrived(sides, has, OPPOSITE)
+        wait_arrived(corners, has_corner, DIAGONAL_OPPOSITE)
+        wait_sent(sides, has)
+        wait_sent(corners, has_corner)
 
     def pack_rows():
         for f in range(3):
@@ -206,6 +245,19 @@
                 tx[b, 1:9, :] = new[b]
         return tx[1, 3:7, :]
 
+    loads[0].wait()
+    pack_rows()
+    count = sum(flag.astype(jnp.int32) for flag in has)
+    pl.semaphore_wait(barrier, count)
+    start(state_copies(0), has, (2, 3, 0, 1))
+    loads[1].wait()
+    eps[...] = jnp.where(ins[...] == 1, 0.4, 1.0).astype(F32)
+    se[0] = eps[pl.ds(0, SIDE, stride=SIDE), :]
+    se[1] = eps[pl.ds(SIDE - 1, SIDE, stride=SIDE), :]
+    start(eps_copies(), has, (2, 3, 0, 1))
+    for copy in loads[2:]:
+        copy.wait()
+
     def lookup(labels, table):
         result = jnp.zeros(labels.shape, F32)
         for level, amount in enumerate(table):
@@ -213,15 +265,18 @@
         return result
 
     for c in range(CELLS):
-        small[4 * c:4 * c + 4, :] = lookup(imp_ref[c], (-2.0, -0.5, 0.5, 2.0))
-        small[16 + 4 * c:16 + 4 * c + 4, :] = lookup(con_ref[c], (0.5, 1.0, 2.0, 4.0))
-        small[32 + 4 * c:32 + 4 * c + 4, :] = war_ref[c]
+        small[4 * c:4 * c + 4, :] = lookup(imp[c], (-2.0, -0.5, 0.5, 2.0))
+        small[16 + 4 * c:16 + 4 * c + 4, :] = lookup(con[c], (0.5, 1.0, 2.0, 4.0))
+        small[32 + 4 * c:32 + 4 * c + 4, :] = war[c]
     zc = LANES // 4
     wide = (lax.broadcasted_iota(jnp.int32, (zc, LANES), 1) // 4 == lax.broadcasted_iota(jnp.int32, (zc, LANES), 0)).astype(F32)
     rep[...] = jnp.dot(small[...], wide, precision=lax.Precision.HIGHEST, preferred_element_type=F32)
     for c in range(CELLS):
         for y in range(CELLS):
-            dop[c, 4 * y:4 * y + 4, :] = jnp.broadcast_to(rep[4 * c + y:4 * c + y + 1, :], (4, LANES))
+            row = jnp.broadcast_to(rep[4 * c + y:4 * c + y + 1, :], (4, LANES))
+            dop[c, 4 * y:4 * y + 4, :] = row
+            if y in (0, CELLS - 1):
+                dopy[y // (CELLS - 1), 4 * c:4 * c + 4, :] = row
 
     def packed(first):
         rows = [rep[pl.ds(first + y, 4, stride=4), :] for y in range(CELLS)]
@@ -234,17 +289,6 @@
     sx[...] = jnp.zeros_like(sx)
     cx[...] = jnp.zeros_like(cx)
     dd[...] = jnp.zeros_like(dd)
-
-    for copy in loads:
-        copy.wait()
-    pack_rows()
-    eps[...] = jnp.where(ins[...] == 1, 0.4, 1.0).astype(F32)
-    se[0] = eps[pl.ds(0, SIDE, stride=SIDE), :]
-    se[1] = eps[pl.ds(SIDE - 1, SIDE, stride=SIDE), :]
-
-    pl.semaphore_wait(barrier, 8)
-    for copy in state_copies(0) + eps_copies() + thermal_copies(0):
-        copy.start()
 
     def weigh(x, below, upper):
         e = eps[slab(x), :]
@@ -295,6 +339,7 @@
 
     def edge(side, mine, halo, weight):
         scale = has[side].astype(F32)
+        halo = [jnp.where(has[side], a, b) for a, b in zip(halo, mine)]
         if side % 2 == 0:
             d, je, jh, gn, gp, g = face(*halo, *mine)
             sign = -scale
@@ -304,6 +349,33 @@
         t = (je - jh) * scale
         return (je * sign, jh * sign, weight * d * sign, d * sign, gn * scale, gp * scale, g * scale), t * t
 
+    def newton(state, sums, faces, mu, level, contact):
+        psi, n, p = state
+        fe, fh, lap, ls, gn, gp, gs = sums
+        rd = 1.0 / (n + p + 2.0)
+        rec = (n * p - 1.0) * rd
+        rn, rp = (p + 1.0) * rd, (n + 1.0) * rd
+        rn, rp = rn * rn, rp * rp
+        r0 = lap + CHARGE * (p - n + level)
+        r1 = mu * fe - rec
+        r2 = mu * fh - rec
+        aa = -faces
+        ba, ca = mu * gn, mu * gp
+        bb = -mu * (gs + 0.5 * ls) - rn - SHIFT
+        cc = -mu * (gs - 0.5 * ls) - rp - SHIFT
+        bc, cb = -rp, -rn
+        c_aa = bb * cc - bc * cb
+        c_ab = bc * ca - ba * cc
+        c_ac = ba * cb - bb * ca
+        inv = 1.0 / (aa * c_aa + CHARGE * (c_ac - c_ab))
+        d0 = (c_aa * r0 + CHARGE * ((cb + cc) * r1 - (bc + bb) * r2)) * inv
+        d1 = (c_ab * r0 + (aa * cc - CHARGE * ca) * r1 + (CHARGE * ba - aa * bc) * r2) * inv
+        d2 = (c_ac * r0 - (CHARGE * ca + aa * cb) * r1 + (aa * bb + CHARGE * ba) * r2) * inv
+        d0 = jnp.where(contact, psi - BIAS * level, d0)
+        d1 = jnp.where(contact, n - 1.0, d1)
+        d2 = jnp.where(contact, p - 1.0, d2)
+        return psi - d0, n * jnp.exp(-d1 / n), p * jnp.exp(-d2 / p)
+
     def step(k, nothing):
         hs[...] = jnp.zeros_like(hs)
         none = (zero,) * 8
@@ -312,24 +384,27 @@
 
         @pl.when(k == 0)
         def _():
-            for copy in eps_copies() + thermal_copies(0):
-                copy.wait()
+            wait_arrived(eps_copies(), has, OPPOSITE)
+            wait_sent(eps_copies(), has)
             for s in range(2):
                 rows = pl.ds(s * (NODES - SIDE), SIDE)
-                wbx[s] = eps[rows, :] + hex_[s]
-                fc[rows, :] = fc[rows, :] + wbx[s] * has[s].astype(F32)
+                wbx[s] = keep(has[s], eps[rows, :] + hex_[s])
+                fc[rows, :] = fc[rows, :] + wbx[s]
             for s in range(2):
                 rows = pl.ds(s * (SIDE - 1), SIDE, stride=SIDE)
-                wby[s] = se[s] + hex_[2 + s]
-                fc[rows, :] = fc[rows, :] + wby[s] * has[2 + s].astype(F32)
+                wby[s] = keep(has[2 + s], se[s] + hex_[2 + s])
+                fc[rows, :] = fc[rows, :] + wby[s]
+
+        @pl.when(k == 1)
+        def _():
+            wait_thermal(0)
             load_corners(0)
             gather_source(0, cx)
             ix[...] = 1.0 / (SINK + 6.0 * cx[...])
 
         @pl.when(k > 0)
         def _():
-            for copy in thermal_copies(k):
-                copy.wait()
+            wait_thermal(k)
             ts[k + 1, 0:4, :] = relax(k)
 
         warm = ts[k + 1, 0:4, :]
@@ -338,10 +413,13 @@
         rep[0:16, :] = m4
         for c in range(CELLS):
             for y in range(CELLS):
-                mob[c, 4 * y:4 * y + 4, :] = jnp.broadcast_to(rep[4 * y + c:4 * y + c + 1, :], (4, LANES))
-
-        for copy in state_copies(k):
-            copy.wait()
+                row = jnp.broadcast_to(rep[4 * y + c:4 * y + c + 1, :], (4, LANES))
+                mob[c, 4 * y:4 * y + 4, :] = row
+                if y in (0, CELLS - 1):
+                    moby[y // (CELLS - 1), 4 * c:4 * c + 4, :] = row
+
+        wait_arrived(state_copies(k), has, OPPOSITE)
+        wait_sent(state_copies(k), has)
         for s in range(2):
             rows = pl.ds(s * (NODES - SIDE), SIDE)
             mine = [st[f, rows, :] for f in range(3)]
@@ -354,9 +432,19 @@
             rows = pl.ds(s * (SIDE - 1), SIDE, stride=SIDE)
             mine = [sy[s, f] for f in range(3)]
             sums, heat = edge(2 + s, mine, [hy[k, s, f] for f in range(3)], wby[s])
+            sums = [acc[q, rows, :] + sums[q] for q in range(7)]
             for q in range(7):
-                acc[q, rows, :] = acc[q, rows, :] + sums[q]
+                acc[q, rows, :] = sums[q]
             yq[s] = heat / (mine[1] + mine[2])
+            new = newton(mine, sums, fc[rows, :], moby[s], dopy[s], ele[rows, :] == 1)
+            for f in range(3):
+                sy[s, f] = new[f]
+
+        following = jnp.minimum(k + 1, NEWTON - 1)
+
+        @pl.when(k < NEWTON - 1)
+        def _():
+            start(state_copies(following), has, (2, 3))
 
         parts = []
         for y in range(CELLS):
@@ -371,59 +459,38 @@
         r = [rep[4 * y:4 * y + 4, :] for y in range(CELLS)]
         heat = jnp.where(lane4 == 0, r[0], jnp.where(lane4 == 1, r[1], jnp.where(lane4 == 2, r[2], r[3])))
         pack_thermal(k + 1, warm, heat * m * (HEAT_GAIN * 0.5 / 64.0))
-        for copy in thermal_copies(k + 1):
-            copy.start()
+        start_thermal(k + 1)
 
         def solve(x, nothing):
             rows = slab(x)
-            psi, n, p = (st[f, rows, :] for f in range(3))
-            fe, fh, lap, ls, gn, gp, gs = (acc[q, rows, :] for q in range(7))
             cell = x // CELLS
-            mu, level = mob[cell], dop[cell]
-            contact = ele[rows, :] == 1
-            rd = 1.0 / (n + p + 2.0)
-            rec = (n * p - 1.0) * rd
-            rn, rp = (p + 1.0) * rd, (n + 1.0) * rd
-            rn, rp = rn * rn, rp * rp
-            r0 = lap + CHARGE * (p - n + level)
-            r1 = mu * fe - rec
-            r2 = mu * fh - rec
-            aa = -fc[rows, :]
-            ba, ca = mu * gn, mu * gp
-            bb = -mu * (gs + 0.5 * ls) - rn - SHIFT
-            cc = -mu * (gs - 0.5 * ls) - rp - SHIFT
-            bc, cb = -rp, -rn
-            c_aa = bb * cc - bc * cb
-            c_ab = bc * ca - ba * cc
-            c_ac = ba * cb - bb * ca
-            inv = 1.0 / (aa * c_aa + CHARGE * (c_ac - c_ab))
-            d0 = (c_aa * r0 + CHARGE * ((cb + cc) * r1 - (bc + bb) * r2)) * inv
-            d1 = (c_ab * r0 + (aa * cc - CHARGE * ca) * r1 + (CHARGE * ba - aa * bc) * r2) * inv
-            d2 = (c_ac * r0 - (CHARGE * ca + aa * cb) * r1 + (aa * bb + CHARGE * ba) * r2) * inv
-            d0 = jnp.where(contact, psi - BIAS * level, d0)
-            d1 = jnp.where(contact, n - 1.0, d1)
-            d2 = jnp.where(contact, p - 1.0, d2)
-            st[0, rows, :] = psi - d0
-            st[1, rows, :] = n * jnp.exp(-d1 / n)
-            st[2, rows, :] = p * jnp.exp(-d2 / p)
+            new = newton(
+                [st[f, rows, :] for f in range(3)], [acc[q, rows, :] for q in range(7)],
+                fc[rows, :], mob[cell], dop[cell], ele[rows, :] == 1,
+            )
+            for f in range(3):
+                st[f, rows, :] = new[f]
             return nothing
 
-        lax.fori_loop(0, SIDE, solve, 0)
+        solve(0, 0)
+        solve(SIDE - 1, 0)
 
         @pl.when(k < NEWTON - 1)
         def _():
-            pack_rows()
-            for copy in state_copies(k + 1):
-                copy.start()
-
+            start(state_copies(following), has, (0, 1))
+
+        @pl.when(k == 0)
+        def _():
+            start_thermal(0)
+
+        lax.fori_loop(1, SIDE - 1, solve, 0)
         return nothing
 
     lax.fori_loop(0, NEWTON, step, 0)
 
     store = pltpu.make_async_copy(st, out_ref, store_sem)
     store.start()
-    for copy in thermal_copies(NEWTON):
-        copy.wait()
+    wait_thermal(NEWTON)
     warm = relax(NEWTON)
     cells = jnp.concatenate([jnp.where(lane4 == y, warm, 0.0) for y in range(CELLS)], 0)
     narrow = (lax.broadcasted_iota(jnp.int32, (LANES, zc), 0) // 4 == lax.broadcasted_iota(jnp.int32, (LANES, zc), 1)).astype(F32)
@@ -447,13 +514,16 @@
                 jax.ShapeDtypeStruct((3, NODES, LANES), F32),
                 jax.ShapeDtypeStruct((CELLS, CELLS, LANES // 4), F32),
             ),
-            in_specs=[pl.BlockSpec(memory_space=pl.ANY)] * 3 + [pl.BlockSpec(memory_space=pltpu.VMEM)] * 3,
+            in_specs=[pl.BlockSpec(memory_space=pl.ANY)] * 6,
             out_specs=(pl.BlockSpec(memory_space=pl.ANY), pl.BlockSpec(memory_space=pltpu.VMEM)),
             scratch_shapes=[
                 vm((3, NODES, LANES), F32),
                 vm((NODES, LANES), F32),
                 vm((NODES, LANES), jnp.int32),
                 vm((NODES, LANES), jnp.int32),
+                vm((CELLS, CELLS, LANES // 4), jnp.int32),
+                vm((CELLS, CELLS, LANES // 4), jnp.int32),
+                vm((CELLS, CELLS, LANES // 4), F32),
                 vm((3, NODES, LANES), F32),
                 vm((NODES, LANES), F32),
                 vm((7, NODES, LANES), F32),
@@ -461,6 +531,8 @@
                 vm((2,) + tile, F32),
                 vm((CELLS,) + tile, F32),
                 vm((CELLS,) + tile, F32),
+                vm((2,) + tile, F32),
+                vm((2,) + tile, F32),
                 vm((48, LANES), F32),
                 vm((48, LANES // 4), F32),
                 vm((2,) + tile, F32),
@@ -479,7 +551,7 @@
                 vm((3, 8, LANES), F32),
                 vm((3, 8, LANES), F32),
                 vm((8, LANES), F32),
-                dma((3,)),
+                dma((6,)),
                 dma,
                 dma((NEWTON, 4)),
                 dma((NEWTON, 4)),

time: 47.4 us -> 41.5 us (0.88)
  the two profiles are of different devices: /device:TPU:9 before, /device:TPU:15 now
where the time goes in v2:
time: 41.5 us; the launch traced here: 41.3 us
  Pallas kernels  38.2 us (92%)
  local copies, waits for them, and re-layouts  2.37 us (6%)
  between operations  0.65 us (2%)
    pallas_call x1, Pallas kernels, per_device(): call(sol.reshape(3, NODES, LANES), ins.reshape(NODES, LANES), ele.reshape...  38.2 us
    unnamed x4, local copies, waits for them, and re-layouts  2.37 us

profile of v2, /device:TPU:15, one launch (start us, length us, event | category | flops | bytes accessed | tf_op | source)
XLA Modules:
  0.0 41.3 jit_solution(18227951004716409715)
XLA Ops:
  0.6 38.2 %shard_map.77 = (f32[3,256,128]{2,1,0:T(8,128)}, f32[4,4,32]{2,1,0:T(4,128)}) custom-call(f32[3,256,128]{2,1,0:T(8,128)} %bitcast.5, s32[256,128]{1,0:T(8,128)} %bitcast.6, s32[256,128]{1,0:T(8,128)} %bitcast.7, s32[4,4,32]{2,1,0:T(4,128)} %imp_ref.1, s32[4,4,32]{2,1,0:T(4,128)} %con_ref.1, f32[4,4,32]{2,1,0:T(4,128)} %war_ref.1), custom_call_target="tpu_custom_call" | custom-call | tf_op jit(solution)/shard_map/pallas_call | solution.py:567
  38.9 0.0 copy-start
  38.9 1.8 %copy.10 = f32[3,16,16,128]{3,2,1,0:T(8,128)} copy(f32[3,16,16,128]{3,2,1,0:T(8,128)} %bitcast.4) | data formatting | bytes 786432
  40.7 0.0 copy-done
  40.7 0.6 %copy.11 = f32[4,4,32]{2,1,0:T(4,128)} copy(f32[4,4,32]{2,1,0:T(4,128)S(1)} %copy-done) | data formatting | bytes 4096
Async XLA Ops:
  38.9 1.8 %copy-start = (f32[4,4,32]{2,1,0:T(4,128)S(1)}, f32[4,4,32]{2,1,0:T(4,128)}, u32[]{:S(2)}) copy-start(f32[4,4,32]{2,1,0:T(4,128)} %get-tuple-element.9) | copy-start | bytes 6148

commit v3 on v2

--- a/solution.py
+++ b/solution.py
@@ -57,10 +57,10 @@
 def body(
     nx, ny,
     sol_ref, ins_ref, ele_ref, imp_ref, con_ref, war_ref,
-    out_ref, temp_ref,
-    st, eps, ins, ele, imp, con, war, wl, fc, acc, hs, yq, mob, dop, moby, dopy, rep, small, wbx, wby,
+    st, temp_ref,
+    eps, ins, ele, imp, con, war, wl, fc, acc, hs, yq, mob, dop, moby, dopy, rep, small, wbx, wby,
     hx, hy, hex_, se, sy, ts, ds, tr, dr, tx, sx, cx, ix, dd,
-    load_sem, store_sem, s_send, s_recv, e_send, e_recv, t_send, t_recv, d_send, d_recv,
+    load_sem, s_send, s_recv, e_send, e_recv, t_send, t_recv, d_send, d_recv,
 ):
     gx = lax.axis_index("gx")
     gy = lax.axis_index("gy")
@@ -488,10 +488,16 @@
 
     lax.fori_loop(0, NEWTON, step, 0)
 
-    store = pltpu.make_async_copy(st, out_ref, store_sem)
+    wait_thermal(NEWTON)
+    temp_ref[0:4, :] = relax(NEWTON)
+
+
+def emit(st_ref, warm_ref, out_ref, temp_ref, sem):
+    store = pltpu.make_async_copy(st_ref, out_ref, sem)
     store.start()
-    wait_thermal(NEWTON)
-    warm = relax(NEWTON)
+    warm = warm_ref[0:4, :]
+    lane4 = lax.broadcasted_iota(jnp.int32, (1, LANES), 1) & 3
+    zc = LANES // 4
     cells = jnp.concatenate([jnp.where(lane4 == y, warm, 0.0) for y in range(CELLS)], 0)
     narrow = (lax.broadcasted_iota(jnp.int32, (LANES, zc), 0) // 4 == lax.broadcasted_iota(jnp.int32, (LANES, zc), 1)).astype(F32)
     cells = jnp.dot(cells, narrow, precision=lax.Precision.HIGHEST, preferred_element_type=F32)
@@ -511,13 +517,12 @@
         call = pl.pallas_call(
             functools.partial(body, nx, ny),
             out_shape=(
-                jax.ShapeDtypeStruct((3, NODES, LANES), F32),
-                jax.ShapeDtypeStruct((CELLS, CELLS, LANES // 4), F32),
+                pltpu.VMEM((3, NODES, LANES), F32),
+                pltpu.VMEM((8, LANES), F32),
             ),
             in_specs=[pl.BlockSpec(memory_space=pl.ANY)] * 6,
-            out_specs=(pl.BlockSpec(memory_space=pl.ANY), pl.BlockSpec(memory_space=pltpu.VMEM)),
+            out_specs=(pl.BlockSpec(memory_space=pltpu.VMEM), pl.BlockSpec(memory_space=pltpu.VMEM)),
             scratch_shapes=[
-                vm((3, NODES, LANES), F32),
                 vm((NODES, LANES), F32),
                 vm((NODES, LANES), jnp.int32),
                 vm((NODES, LANES), jnp.int32),
@@ -552,7 +557,6 @@
                 vm((3, 8, LANES), F32),
                 vm((8, LANES), F32),
                 dma((6,)),
-                dma,
                 dma((NEWTON, 4)),
                 dma((NEWTON, 4)),
                 dma((4,)),
@@ -567,6 +571,18 @@
         state, warm = call(
             sol.reshape(3, NODES, LANES), ins.reshape(NODES, LANES), ele.reshape(NODES, LANES), imp, con, war
         )
+        state = pltpu.with_memory_space_constraint(state, pltpu.VMEM)
+        warm = pltpu.with_memory_space_constraint(warm, pltpu.VMEM)
+        state, warm = pl.pallas_call(
+            emit,
+            out_shape=(
+                jax.ShapeDtypeStruct((3, NODES, LANES), F32),
+                jax.ShapeDtypeStruct((CELLS, CELLS, LANES // 4), F32),
+            ),
+            in_specs=[pl.BlockSpec(memory_space=pltpu.VMEM), pl.BlockSpec(memory_space=pltpu.VMEM)],
+            out_specs=(pl.BlockSpec(memory_space=pl.ANY), pl.BlockSpec(memory_space=pltpu.VMEM)),
+            scratch_shapes=[dma],
+        )(state, warm)
         return state.reshape(3, SIDE, SIDE, LANES), warm
 
     spec = P("gx", "gy", None)

time: 41.5 us -> 39.7 us (0.957)
  local copies, waits for them, and re-layouts: 2.37 us -> 0 us
  Pallas kernels: 38.2 us -> 38.8 us
    unnamed x4 -> x0, local copies, waits for them, and re-layouts: 2.37 us -> none
    pallas_call x0 -> x1, Pallas kernels: none -> 1.35 us  [per_device(): pl.pallas_call(emit, out_shape=(jax.ShapeDtypeStruct((3, NODES, LANES), F...]
    pallas_call x1, Pallas kernels: 38.2 us -> 37.5 us  [per_device(): call(sol.reshape(3, NODES, LANES), ins.reshape(NODES, LANES), ele.reshape...]
where the time goes in v3:
time: 39.7 us; the launch traced here: 39.5 us
  Pallas kernels  38.8 us (98%)
  between operations  0.64 us (2%)
    pallas_call x1, Pallas kernels, per_device(): call(sol.reshape(3, NODES, LANES), ins.reshape(NODES, LANES), ele.reshape...  37.5 us
    pallas_call x1, Pallas kernels, per_device(): pl.pallas_call(emit, out_shape=(jax.ShapeDtypeStruct((3, NODES, LANES), F...  1.35 us

profile of v3, /device:TPU:15, one launch (start us, length us, event | category | flops | bytes accessed | tf_op | source)
XLA Modules:
  0.0 39.5 jit_solution(15062863309167456135)
XLA Ops:
  0.6 37.5 %shard_map.77 = (f32[3,256,128]{2,1,0:T(8,128)S(1)}, f32[8,128]{1,0:T(8,128)S(1)}) custom-call(f32[3,256,128]{2,1,0:T(8,128)} %bitcast.4, s32[256,128]{1,0:T(8,128)} %bitcast.5, s32[256,128]{1,0:T(8,128)} %bitcast.6, s32[4,4,32]{2,1,0:T(4,128)} %imp_ref.1, s32[4,4,32]{2,1,0:T(4,128)} %con_ref.1, f32[4,4,32]{2,1,0:T(4,128)} %war_ref.1), custom_call_target="tpu_custom_call" | custom-call | tf_op jit(solution)/shard_map/pallas_call | solution.py:571
  38.1 1.4 %shard_map.78 = (f32[3,256,128]{2,1,0:T(8,128)}, f32[4,4,32]{2,1,0:T(4,128)}) custom-call(f32[3,256,128]{2,1,0:T(8,128)S(1)} %get-tuple-element.6.st_ref, f32[8,128]{1,0:T(8,128)S(1)} %get-tuple-element.7.warm_ref), custom_call_target="tpu_custom_call" | custom-call | tf_op jit(solution)/shard_map/pallas_call | solution.py:576

commit v4 on v3

--- a/solution.py
+++ b/solution.py
@@ -58,9 +58,9 @@
     nx, ny,
     sol_ref, ins_ref, ele_ref, imp_ref, con_ref, war_ref,
     st, temp_ref,
-    eps, ins, ele, imp, con, war, wl, fc, acc, hs, yq, mob, dop, moby, dopy, rep, small, wbx, wby,
-    hx, hy, hex_, se, sy, ts, ds, tr, dr, tx, sx, cx, ix, dd,
-    load_sem, s_send, s_recv, e_send, e_recv, t_send, t_recv, d_send, d_recv,
+    eps, ins, ele, imp, con, war, wl, fc, acc, hs, qe, hin, mob, dop, mobb, dopb, fcb, eleb, rep, small, wb,
+    hb, hex_, se, sb, cs, cr, ts, ds, tr, dr, tx, sx, cx, ix, dd,
+    load_sem, s_send, s_recv, e_send, e_recv, c_send, c_recv, t_send, t_recv, d_send, d_recv,
 ):
     gx = lax.axis_index("gx")
     gy = lax.axis_index("gy")
@@ -91,6 +91,7 @@
 
     lane = lax.broadcasted_iota(jnp.int32, (1, LANES), 1)
     lane4 = lane & 3
+    tile_shape = (SIDE, LANES)
     last_lane = (lane != LANES - 1).astype(F32)
     last_row = (lax.broadcasted_iota(jnp.int32, (SIDE, LANES), 0) != SIDE - 1).astype(F32)
 
@@ -124,22 +125,16 @@
                 copies[opposite[s]].wait_recv()
 
     def state_copies(k):
-        out = []
-        for s in range(4):
-            if s < 2:
-                src = st.at[:, pl.ds(0 if s == 0 else NODES - SIDE, SIDE), :]
-                dst = hx.at[k, OPPOSITE[s]]
-            else:
-                src, dst = sy.at[s - 2], hy.at[k, OPPOSITE[s] - 2]
-            out.append(remote(src, dst, s_send.at[k, s], s_recv.at[k, OPPOSITE[s]], near[s]))
-        return out
+        return [
+            remote(sb.at[k, s], hb.at[k, OPPOSITE[s]], s_send.at[k, s], s_recv.at[k, OPPOSITE[s]], near[s])
+            for s in range(4)
+        ]
 
     def eps_copies():
-        out = []
-        for s in range(4):
-            src = eps.at[pl.ds(0 if s == 0 else NODES - SIDE, SIDE), :] if s < 2 else se.at[s - 2]
-            out.append(remote(src, hex_.at[OPPOSITE[s]], e_send.at[s], e_recv.at[OPPOSITE[s]], near[s]))
-        return out
+        return [remote(se.at[s], hex_.at[OPPOSITE[s]], e_send.at[s], e_recv.at[OPPOSITE[s]], near[s]) for s in range(4)]
+
+    def cond_copies():
+        return [remote(cs, cr.at[OPPOSITE[s]], c_send.at[s], c_recv.at[OPPOSITE[s]], near[s]) for s in range(4)]
 
     def thermal_copies(t):
         sides, corners = [], []
@@ -153,20 +148,23 @@
 
     def start_thermal(t):
         sides, corners = thermal_copies(t)
+        start(sides, has, (2, 3))
         start(corners, has_corner, range(4))
-        start(sides, has, (2, 3, 0, 1))
+        start(sides, has, (0, 1))
 
     def wait_thermal(t):
         sides, corners = thermal_copies(t)
         wait_arrived(sides, has, OPPOSITE)
         wait_arrived(corners, has_corner, DIAGONAL_OPPOSITE)
+
+    def wait_thermal_sent(t):
+        sides, corners = thermal_copies(t)
         wait_sent(sides, has)
         wait_sent(corners, has_corner)
 
-    def pack_rows():
-        for f in range(3):
-            sy[0, f] = st[f, pl.ds(0, SIDE, stride=SIDE), :]
-            sy[1, f] = st[f, pl.ds(SIDE - 1, SIDE, stride=SIDE), :]
+    border = (
+        pl.ds(0, SIDE), pl.ds(NODES - SIDE, SIDE), pl.ds(0, SIDE, stride=SIDE), pl.ds(SIDE - 1, SIDE, stride=SIDE)
+    )
 
     def pack_thermal(t, warm, source):
         ts[t, 0:4, :] = warm
@@ -181,17 +179,17 @@
         def high(a, b):
             return jnp.where(lane4 >= 2, tile[a:a + 1], jnp.where(lane4 == 1, down2[b:b + 1], down3[a + 4:a + 5]))
 
-        ds[t, 0] = low(0, 1)
-        ds[t, 1] = high(0, 1)
-        ds[t, 2] = low(3, 2)
-        ds[t, 3] = high(3, 2)
+        ds[t, 0, 0:1, :] = low(0, 1)
+        ds[t, 1, 0:1, :] = high(0, 1)
+        ds[t, 2, 0:1, :] = low(3, 2)
+        ds[t, 3, 0:1, :] = high(3, 2)
 
     def keep(flag, a):
         return jnp.where(flag, a, jnp.zeros_like(a))
 
     def load_corners(t):
         for s in range(4):
-            dd[s:s + 1, :] = keep(has_corner[s], dr[t, s])
+            dd[s:s + 1, :] = keep(has_corner[s], dr[t, s, 0:1, :])
 
     def gather_source(t, into):
         tile = dd[...]
@@ -245,18 +243,15 @@
                 tx[b, 1:9, :] = new[b]
         return tx[1, 3:7, :]
 
-    loads[0].wait()
-    pack_rows()
-    count = sum(flag.astype(jnp.int32) for flag in has)
-    pl.semaphore_wait(barrier, count)
-    start(state_copies(0), has, (2, 3, 0, 1))
-    loads[1].wait()
+    for copy in loads:
+        copy.wait()
+    for s in range(4):
+        for f in range(3):
+            sb[0, s, f] = st[f, border[s], :]
     eps[...] = jnp.where(ins[...] == 1, 0.4, 1.0).astype(F32)
-    se[0] = eps[pl.ds(0, SIDE, stride=SIDE), :]
-    se[1] = eps[pl.ds(SIDE - 1, SIDE, stride=SIDE), :]
-    start(eps_copies(), has, (2, 3, 0, 1))
-    for copy in loads[2:]:
-        copy.wait()
+    for s in range(4):
+        se[s] = eps[border[s], :]
+        eleb[s] = ele[border[s], :]
 
     def lookup(labels, table):
         result = jnp.zeros(labels.shape, F32)
@@ -275,20 +270,33 @@
         for y in range(CELLS):
             row = jnp.broadcast_to(rep[4 * c + y:4 * c + y + 1, :], (4, LANES))
             dop[c, 4 * y:4 * y + 4, :] = row
+            if c in (0, CELLS - 1):
+                dopb[c // (CELLS - 1), 4 * y:4 * y + 4, :] = row
             if y in (0, CELLS - 1):
-                dopy[y // (CELLS - 1), 4 * c:4 * c + 4, :] = row
+                dopb[2 + y // (CELLS - 1), 4 * c:4 * c + 4, :] = row
 
     def packed(first):
         rows = [rep[pl.ds(first + y, 4, stride=4), :] for y in range(CELLS)]
         return jnp.where(lane4 == 0, rows[0], jnp.where(lane4 == 1, rows[1], jnp.where(lane4 == 2, rows[2], rows[3])))
 
     cond, warm0 = packed(16), packed(32)
-    pack_thermal(0, cond, cond)
+    cs[0:4, :] = cond
+    cs[4:8, :] = cond
+    ds[...] = jnp.zeros_like(ds)
+    for s in range(4):
+        at = (s // 2) * (CELLS - 1)
+        ds[1, s, 1:2, :] = cs[at:at + 1, :]
     ts[1, 0:4, :] = warm0
     tx[...] = jnp.zeros_like(tx)
     sx[...] = jnp.zeros_like(sx)
     cx[...] = jnp.zeros_like(cx)
     dd[...] = jnp.zeros_like(dd)
+
+    count = sum(flag.astype(jnp.int32) for flag in has)
+    pl.semaphore_wait(barrier, count)
+    start(state_copies(0), has, (2, 3, 0, 1))
+    start(eps_copies(), has, (2, 3, 0, 1))
+    start(cond_copies(), has, (2, 3, 0, 1))
 
     def weigh(x, below, upper):
         e = eps[slab(x), :]
@@ -337,18 +345,6 @@
         hs[cell, :] = hs[cell, :] + sums[7] / (n + p)
         return carry
 
-    def edge(side, mine, halo, weight):
-        scale = has[side].astype(F32)
-        halo = [jnp.where(has[side], a, b) for a, b in zip(halo, mine)]
-        if side % 2 == 0:
-            d, je, jh, gn, gp, g = face(*halo, *mine)
-            sign = -scale
-        else:
-            d, je, jh, gn, gp, g = face(*mine, *halo)
-            sign = scale
-        t = (je - jh) * scale
-        return (je * sign, jh * sign, weight * d * sign, d * sign, gn * scale, gp * scale, g * scale), t * t
-
     def newton(state, sums, faces, mu, level, contact):
         psi, n, p = state
         fe, fh, lap, ls, gn, gp, gs = sums
@@ -376,90 +372,114 @@
         d2 = jnp.where(contact, p - 1.0, d2)
         return psi - d0, n * jnp.exp(-d1 / n), p * jnp.exp(-d2 / p)
 
+    def pick(rows):
+        return jnp.where(lane4 == 0, rows[0], jnp.where(lane4 == 1, rows[1], jnp.where(lane4 == 2, rows[2], rows[3])))
+
+    def stack(ref, *index):
+        return jnp.concatenate([ref[index[:1] + (s,) + index[1:]] if len(index) > 1 else ref[s] for s in range(4)], 0)
+
     def step(k, nothing):
+        following = jnp.minimum(k + 1, NEWTON - 1)
+
         hs[...] = jnp.zeros_like(hs)
         none = (zero,) * 8
         below = lax.fori_loop(0, SIDE - 1, lambda x, b: fluxes(x, b, True), none)
         fluxes(SIDE - 1, below, False)
-
-        @pl.when(k == 0)
-        def _():
-            wait_arrived(eps_copies(), has, OPPOSITE)
-            wait_sent(eps_copies(), has)
-            for s in range(2):
-                rows = pl.ds(s * (NODES - SIDE), SIDE)
-                wbx[s] = keep(has[s], eps[rows, :] + hex_[s])
-                fc[rows, :] = fc[rows, :] + wbx[s]
-            for s in range(2):
-                rows = pl.ds(s * (SIDE - 1), SIDE, stride=SIDE)
-                wby[s] = keep(has[2 + s], se[s] + hex_[2 + s])
-                fc[rows, :] = fc[rows, :] + wby[s]
-
-        @pl.when(k == 1)
-        def _():
-            wait_thermal(0)
-            load_corners(0)
-            gather_source(0, cx)
-            ix[...] = 1.0 / (SINK + 6.0 * cx[...])
-
-        @pl.when(k > 0)
-        def _():
-            wait_thermal(k)
-            ts[k + 1, 0:4, :] = relax(k)
-
-        warm = ts[k + 1, 0:4, :]
-        m = 1.0 / (1.0 + DROP * warm)
-        m4 = spread(jnp.concatenate([jnp.where(lane4 == y, m, 0.0) for y in range(CELLS)], 0), lane)
-        rep[0:16, :] = m4
-        for c in range(CELLS):
-            for y in range(CELLS):
-                row = jnp.broadcast_to(rep[4 * y + c:4 * y + c + 1, :], (4, LANES))
-                mob[c, 4 * y:4 * y + 4, :] = row
-                if y in (0, CELLS - 1):
-                    moby[y // (CELLS - 1), 4 * c:4 * c + 4, :] = row
-
-        wait_arrived(state_copies(k), has, OPPOSITE)
-        wait_sent(state_copies(k), has)
-        for s in range(2):
-            rows = pl.ds(s * (NODES - SIDE), SIDE)
-            mine = [st[f, rows, :] for f in range(3)]
-            sums, heat = edge(s, mine, [hx[k, s, f] for f in range(3)], wbx[s])
-            for q in range(7):
-                acc[q, rows, :] = acc[q, rows, :] + sums[q]
-            cell = pl.ds(s * (64 - SIDE), SIDE)
-            hs[cell, :] = hs[cell, :] + heat / (mine[1] + mine[2])
-        for s in range(2):
-            rows = pl.ds(s * (SIDE - 1), SIDE, stride=SIDE)
-            mine = [sy[s, f] for f in range(3)]
-            sums, heat = edge(2 + s, mine, [hy[k, s, f] for f in range(3)], wby[s])
-            sums = [acc[q, rows, :] + sums[q] for q in range(7)]
-            for q in range(7):
-                acc[q, rows, :] = sums[q]
-            yq[s] = heat / (mine[1] + mine[2])
-            new = newton(mine, sums, fc[rows, :], moby[s], dopy[s], ele[rows, :] == 1)
-            for f in range(3):
-                sy[s, f] = new[f]
-
-        following = jnp.minimum(k + 1, NEWTON - 1)
-
-        @pl.when(k < NEWTON - 1)
-        def _():
-            start(state_copies(following), has, (2, 3))
-
         parts = []
         for y in range(CELLS):
             total = hs[pl.ds(4 * y, 4, stride=SIDE), :]
             for i in range(1, 4):
                 total = total + hs[pl.ds(4 * y + i, 4, stride=SIDE), :]
-            if y in (0, CELLS - 1):
-                for i in range(4):
-                    total = total + yq[y // (CELLS - 1), pl.ds(i, 4, stride=4), :]
             parts.append(total)
         rep[0:16, :] = spread(jnp.concatenate(parts, 0), lane)
-        r = [rep[4 * y:4 * y + 4, :] for y in range(CELLS)]
-        heat = jnp.where(lane4 == 0, r[0], jnp.where(lane4 == 1, r[1], jnp.where(lane4 == 2, r[2], r[3])))
-        pack_thermal(k + 1, warm, heat * m * (HEAT_GAIN * 0.5 / 64.0))
+        hin[0:4, :] = pick([rep[4 * y:4 * y + 4, :] for y in range(CELLS)])
+
+        @pl.when(k == 1)
+        def _():
+            wait_thermal(1)
+            for s, (b, r) in enumerate(((0, 1), (2, 1), (0, 6), (2, 6))):
+                cx[b, r:r + 1, :] = keep(has_corner[s], dr[1, s, 1:2, :])
+            ix[...] = 1.0 / (SINK + 6.0 * cx[...])
+
+        @pl.when(k > 1)
+        def _():
+            wait_thermal(k)
+
+        @pl.when(k > 0)
+        def _():
+            ts[k + 1, 0:4, :] = relax(k)
+
+        warm = ts[k + 1, 0:4, :]
+        m = 1.0 / (1.0 + DROP * warm)
+
+        wait_arrived(state_copies(k), has, OPPOSITE)
+        mine = [stack(sb, k, f) for f in range(3)]
+        scale = jnp.concatenate([jnp.broadcast_to(flag.astype(F32), tile_shape) for flag in has], 0)
+        halo = [jnp.where(scale > 0.0, stack(hb, k, f), own) for f, own in enumerate(mine)]
+        d, je, jh, gn, gp, g = face(*mine, *halo)
+        t = (je - jh) * scale
+        qe[...] = t * t / (mine[1] + mine[2])
+        edge = qe[pl.ds(0, 16, stride=4), :]
+        for i in range(1, 4):
+            edge = edge + qe[pl.ds(i, 16, stride=4), :]
+        rep[0:16, :] = spread(edge, lane)
+        heat = hin[0:4, :] + jnp.where(lane4 == 0, rep[8:12, :], jnp.where(lane4 == 3, rep[12:16, :], 0.0))
+        hin[0:4, :] = heat
+        for c in range(2):
+            at = c * (CELLS - 1)
+            hin[at:at + 1, :] = hin[at:at + 1, :] + pick([rep[4 * c + y:4 * c + y + 1, :] for y in range(CELLS)])
+        pack_thermal(k + 1, warm, hin[0:4, :] * m * (HEAT_GAIN * 0.5 / 64.0))
         start_thermal(k + 1)
+
+        @pl.when(k == 0)
+        def _():
+            wait_arrived(eps_copies(), has, OPPOSITE)
+            for s in range(4):
+                wb[s] = keep(has[s], se[s] + hex_[s])
+                fc[border[s], :] = fc[border[s], :] + wb[s]
+            for s in range(4):
+                fcb[s] = fc[border[s], :]
+
+        sums = (je * scale, jh * scale, stack(wb) * d, d * scale, gn * scale, gp * scale, g * scale)
+        for s in range(4):
+            for q in range(7):
+                acc[q, border[s], :] = acc[q, border[s], :] + sums[q][SIDE * s:SIDE * s + SIDE]
+        m4 = spread(jnp.concatenate([jnp.where(lane4 == y, m, 0.0) for y in range(CELLS)], 0), lane)
+        rep[0:16, :] = m4
+        for a in range(2):
+            at = a * (CELLS - 1)
+            for b in range(CELLS):
+                mobb[a, 4 * b:4 * b + 4, :] = jnp.broadcast_to(rep[4 * b + at:4 * b + at + 1, :], (4, LANES))
+                mobb[2 + a, 4 * b:4 * b + 4, :] = jnp.broadcast_to(rep[4 * at + b:4 * at + b + 1, :], (4, LANES))
+
+        @pl.when(k < NEWTON - 1)
+        def _():
+            for pair in ((2, 3), (0, 1)):
+                new = []
+                for s in pair:
+                    new.append(newton(
+                        [sb[k, s, f] for f in range(3)], [acc[q, border[s], :] for q in range(7)],
+                        fcb[s], mobb[s], dopb[s], eleb[s] == 1,
+                    ))
+                for s, values in zip(pair, new):
+                    for f in range(3):
+                        sb[following, s, f] = values[f]
+                start(state_copies(following), has, pair)
+
+        for c in range(CELLS):
+            for y in range(CELLS):
+                mob[c, 4 * y:4 * y + 4, :] = jnp.broadcast_to(rep[4 * y + c:4 * y + c + 1, :], (4, LANES))
+
+        @pl.when(k == 0)
+        def _():
+            wait_sent(eps_copies(), has)
+            wait_sent(cond_copies(), has)
+            wait_arrived(cond_copies(), has, OPPOSITE)
+            cx[1, 0:2, :] = keep(has[0], cr[0, 2:4, :])
+            cx[1, 2:6, :] = cs[0:4, :]
+            cx[1, 6:8, :] = keep(has[1], cr[1, 0:2, :])
+            cx[0, 2:6, :] = keep(has[2], cr[2, 0:4, :])
+            cx[2, 2:6, :] = keep(has[3], cr[3, 0:4, :])
 
         def solve(x, nothing):
             rows = slab(x)
@@ -472,28 +492,24 @@
                 st[f, rows, :] = new[f]
             return nothing
 
-        solve(0, 0)
-        solve(SIDE - 1, 0)
-
-        @pl.when(k < NEWTON - 1)
-        def _():
-            start(state_copies(following), has, (0, 1))
-
-        @pl.when(k == 0)
-        def _():
-            start_thermal(0)
-
-        lax.fori_loop(1, SIDE - 1, solve, 0)
+        lax.fori_loop(0, SIDE, solve, 0)
+        wait_sent(state_copies(k), has)
+
+        @pl.when(k > 0)
+        def _():
+            wait_thermal_sent(k)
+
         return nothing
 
     lax.fori_loop(0, NEWTON, step, 0)
 
     wait_thermal(NEWTON)
     temp_ref[0:4, :] = relax(NEWTON)
-
-
-def emit(st_ref, warm_ref, out_ref, temp_ref, sem):
-    store = pltpu.make_async_copy(st_ref, out_ref, sem)
+    wait_thermal_sent(NEWTON)
+
+
+def emit(st_ref, warm_ref, out_ref, temp_out, temp_ref, sem):
+    store = pltpu.make_async_copy(st_ref, out_ref, sem.at[0])
     store.start()
     warm = warm_ref[0:4, :]
     lane4 = lax.broadcasted_iota(jnp.int32, (1, LANES), 1) & 3
@@ -504,7 +520,10 @@
     for c in range(CELLS):
         for y in range(CELLS):
             temp_ref[c, y:y + 1, :] = cells[4 * y + c:4 * y + c + 1, :]
+    last = pltpu.make_async_copy(temp_ref, temp_out, sem.at[1])
+    last.start()
     store.wait()
+    last.wait()
 
 
 def solution(mesh):
@@ -533,24 +552,27 @@
                 vm((NODES, LANES), F32),
                 vm((7, NODES, LANES), F32),
                 vm((64, LANES), F32),
-                vm((2,) + tile, F32),
+                vm((64, LANES), F32),
+                vm((8, LANES), F32),
                 vm((CELLS,) + tile, F32),
                 vm((CELLS,) + tile, F32),
-                vm((2,) + tile, F32),
-                vm((2,) + tile, F32),
+                vm((4,) + tile, F32),
+                vm((4,) + tile, F32),
+                vm((4,) + tile, F32),
+                vm((4,) + tile, jnp.int32),
                 vm((48, LANES), F32),
                 vm((48, LANES // 4), F32),
-                vm((2,) + tile, F32),
-                vm((2,) + tile, F32),
-                vm((NEWTON, 2, 3) + tile, F32),
-                vm((NEWTON, 2, 3) + tile, F32),
                 vm((4,) + tile, F32),
-                vm((2,) + tile, F32),
-                vm((2, 3) + tile, F32),
+                vm((NEWTON, 4, 3) + tile, F32),
+                vm((4,) + tile, F32),
+                vm((4,) + tile, F32),
+                vm((NEWTON, 4, 3) + tile, F32),
+                vm((8, LANES), F32),
+                vm((4, 8, LANES), F32),
                 vm((NEWTON + 1, 8, LANES), F32),
-                vm((NEWTON + 1, 4, 1, LANES), F32),
+                vm((NEWTON + 1, 4, 2, LANES), F32),
                 vm((NEWTON + 1, 4, 8, LANES), F32),
-                vm((NEWTON + 1, 4, 1, LANES), F32),
+                vm((NEWTON + 1, 4, 2, LANES), F32),
                 vm((3, SIDE, LANES), F32),
                 vm((3, 8, LANES), F32),
                 vm((3, 8, LANES), F32),
@@ -559,6 +581,8 @@
                 dma((6,)),
                 dma((NEWTON, 4)),
                 dma((NEWTON, 4)),
+                dma((4,)),
+                dma((4,)),
                 dma((4,)),
                 dma((4,)),
                 dma((NEWTON + 1, 4)),
@@ -580,8 +604,8 @@
                 jax.ShapeDtypeStruct((CELLS, CELLS, LANES // 4), F32),
             ),
             in_specs=[pl.BlockSpec(memory_space=pltpu.VMEM), pl.BlockSpec(memory_space=pltpu.VMEM)],
-            out_specs=(pl.BlockSpec(memory_space=pl.ANY), pl.BlockSpec(memory_space=pltpu.VMEM)),
-            scratch_shapes=[dma],
+            out_specs=(pl.BlockSpec(memory_space=pl.ANY), pl.BlockSpec(memory_space=pl.ANY)),
+            scratch_shapes=[vm((CELLS, CELLS, LANES // 4), F32), dma((2,))],
         )(state, warm)
         return state.reshape(3, SIDE, SIDE, LANES), warm
 

time: 39.7 us -> 36.1 us (0.909)
  Pallas kernels: 38.8 us -> 35.3 us
    pallas_call x1, Pallas kernels: 37.5 us -> 34.5 us  [per_device(): call(sol.reshape(3, NODES, LANES), ins.reshape(NODES, LANES), ele.reshape...]
    pallas_call x1, Pallas kernels: 1.35 us -> 0.79 us  [per_device(): pl.pallas_call(emit, out_shape=(jax.ShapeDtypeStruct((3, NODES, LANES), F...]
where the time goes in v4:
time: 36.1 us; the launch traced here: 36 us
  Pallas kernels  35.3 us (98%)
  between operations  0.64 us (2%)
    pallas_call x1, Pallas kernels, per_device(): call(sol.reshape(3, NODES, LANES), ins.reshape(NODES, LANES), ele.reshape...  34.5 us
    pallas_call x1, Pallas kernels, per_device(): pl.pallas_call(emit, out_shape=(jax.ShapeDtypeStruct((3, NODES, LANES), F...  0.79 us

profile of v4, /device:TPU:15, one launch (start us, length us, event | category | flops | bytes accessed | tf_op | source)
XLA Modules:
  0.0 36.0 jit_solution(5230278295361379675)
XLA Ops:
  0.6 34.5 %shard_map.77 = (f32[3,256,128]{2,1,0:T(8,128)S(1)}, f32[8,128]{1,0:T(8,128)S(1)}) custom-call(f32[3,256,128]{2,1,0:T(8,128)} %bitcast.4, s32[256,128]{1,0:T(8,128)} %bitcast.5, s32[256,128]{1,0:T(8,128)} %bitcast.6, s32[4,4,32]{2,1,0:T(4,128)} %imp_ref.1, s32[4,4,32]{2,1,0:T(4,128)} %con_ref.1, f32[4,4,32]{2,1,0:T(4,128)} %war_ref.1), custom_call_target="tpu_custom_call" | custom-call | tf_op jit(solution)/shard_map/pallas_call | solution.py:595
  35.2 0.8 %shard_map.78 = (f32[3,256,128]{2,1,0:T(8,128)}, f32[4,4,32]{2,1,0:T(4,128)}) custom-call(f32[3,256,128]{2,1,0:T(8,128)S(1)} %get-tuple-element.6.st_ref, f32[8,128]{1,0:T(8,128)S(1)} %get-tuple-element.7.warm_ref), custom_call_target="tpu_custom_call" | custom-call | tf_op jit(solution)/shard_map/pallas_call | solution.py:600

commit v5 on v4

--- a/solution.py
+++ b/solution.py
@@ -20,6 +20,11 @@
 HEAT_GAIN = 1.0
 SINK = 0.3
 DROP = 0.5
+
+STATE_ROWS = 3 * SIDE
+EPS_AT = STATE_ROWS
+COND_AT = EPS_AT + SIDE
+FIRST_ROWS = COND_AT + 8
 
 F32 = jnp.float32
 MESH = pl.DeviceIdType.MESH
@@ -59,8 +64,8 @@
     sol_ref, ins_ref, ele_ref, imp_ref, con_ref, war_ref,
     st, temp_ref,
     eps, ins, ele, imp, con, war, wl, fc, acc, hs, qe, hin, mob, dop, mobb, dopb, fcb, eleb, rep, small, wb,
-    hb, hex_, se, sb, cs, cr, ts, ds, tr, dr, tx, sx, cx, ix, dd,
-    load_sem, s_send, s_recv, e_send, e_recv, c_send, c_recv, t_send, t_recv, d_send, d_recv,
+    hb, sb, ts, ds, tr, dr, tx, sx, cx, ix, dd,
+    load_sem, s_send, s_recv, t_send, t_recv, d_send, d_recv,
 ):
     gx = lax.axis_index("gx")
     gy = lax.axis_index("gy")
@@ -110,6 +115,14 @@
             def _():
                 copies[s].start()
 
+    def start_state(copies, pair):
+        if pair == (2, 3):
+            start(copies, has, pair)
+            return
+        even = lax.rem(gx, 2) == 0
+        start(copies, (has[0] & even, has[1]), (0, 1))
+        start(copies, (has[0] & jnp.logical_not(even),), (0,))
+
     def wait_sent(copies, flags):
         for s in range(4):
 
@@ -124,17 +137,17 @@
             def _():
                 copies[opposite[s]].wait_recv()
 
-    def state_copies(k):
+    def state_copies(k, rows=STATE_ROWS):
         return [
-            remote(sb.at[k, s], hb.at[k, OPPOSITE[s]], s_send.at[k, s], s_recv.at[k, OPPOSITE[s]], near[s])
+            remote(
+                sb.at[k, s, pl.ds(0, rows), :], hb.at[k, OPPOSITE[s], pl.ds(0, rows), :],
+                s_send.at[k, s], s_recv.at[k, OPPOSITE[s]], near[s],
+            )
             for s in range(4)
         ]
 
-    def eps_copies():
-        return [remote(se.at[s], hex_.at[OPPOSITE[s]], e_send.at[s], e_recv.at[OPPOSITE[s]], near[s]) for s in range(4)]
-
-    def cond_copies():
-        return [remote(cs, cr.at[OPPOSITE[s]], c_send.at[s], c_recv.at[OPPOSITE[s]], near[s]) for s in range(4)]
+    def first_copies():
+        return state_copies(0, FIRST_ROWS)
 
     def thermal_copies(t):
         sides, corners = [], []
@@ -148,9 +161,8 @@
 
     def start_thermal(t):
         sides, corners = thermal_copies(t)
-        start(sides, has, (2, 3))
         start(corners, has_corner, range(4))
-        start(sides, has, (0, 1))
+        start(sides, has, (2, 3, 0, 1))
 
     def wait_thermal(t):
         sides, corners = thermal_copies(t)
@@ -247,10 +259,10 @@
         copy.wait()
     for s in range(4):
         for f in range(3):
-            sb[0, s, f] = st[f, border[s], :]
+            sb[0, s, SIDE * f:SIDE * f + SIDE, :] = st[f, border[s], :]
     eps[...] = jnp.where(ins[...] == 1, 0.4, 1.0).astype(F32)
     for s in range(4):
-        se[s] = eps[border[s], :]
+        sb[0, s, EPS_AT:EPS_AT + SIDE, :] = eps[border[s], :]
         eleb[s] = ele[border[s], :]
 
     def lookup(labels, table):
@@ -280,12 +292,13 @@
         return jnp.where(lane4 == 0, rows[0], jnp.where(lane4 == 1, rows[1], jnp.where(lane4 == 2, rows[2], rows[3])))
 
     cond, warm0 = packed(16), packed(32)
-    cs[0:4, :] = cond
-    cs[4:8, :] = cond
+    for s in range(4):
+        sb[0, s, COND_AT:COND_AT + 4, :] = cond
+        sb[0, s, COND_AT + 4:COND_AT + 8, :] = cond
     ds[...] = jnp.zeros_like(ds)
     for s in range(4):
         at = (s // 2) * (CELLS - 1)
-        ds[1, s, 1:2, :] = cs[at:at + 1, :]
+        ds[1, s, 1:2, :] = sb[0, 0, COND_AT + at:COND_AT + at + 1, :]
     ts[1, 0:4, :] = warm0
     tx[...] = jnp.zeros_like(tx)
     sx[...] = jnp.zeros_like(sx)
@@ -294,9 +307,8 @@
 
     count = sum(flag.astype(jnp.int32) for flag in has)
     pl.semaphore_wait(barrier, count)
-    start(state_copies(0), has, (2, 3, 0, 1))
-    start(eps_copies(), has, (2, 3, 0, 1))
-    start(cond_copies(), has, (2, 3, 0, 1))
+    start_state(first_copies(), (2, 3))
+    start_state(first_copies(), (0, 1))
 
     def weigh(x, below, upper):
         e = eps[slab(x), :]
@@ -376,7 +388,10 @@
         return jnp.where(lane4 == 0, rows[0], jnp.where(lane4 == 1, rows[1], jnp.where(lane4 == 2, rows[2], rows[3])))
 
     def stack(ref, *index):
-        return jnp.concatenate([ref[index[:1] + (s,) + index[1:]] if len(index) > 1 else ref[s] for s in range(4)], 0)
+        if not index:
+            return jnp.concatenate([ref[s] for s in range(4)], 0)
+        k, f = index
+        return jnp.concatenate([ref[k, s, SIDE * f:SIDE * f + SIDE, :] for s in range(4)], 0)
 
     def step(k, nothing):
         following = jnp.minimum(k + 1, NEWTON - 1)
@@ -412,7 +427,14 @@
         warm = ts[k + 1, 0:4, :]
         m = 1.0 / (1.0 + DROP * warm)
 
-        wait_arrived(state_copies(k), has, OPPOSITE)
+        @pl.when(k == 0)
+        def _():
+            wait_arrived(first_copies(), has, OPPOSITE)
+
+        @pl.when(k > 0)
+        def _():
+            wait_arrived(state_copies(k), has, OPPOSITE)
+
         mine = [stack(sb, k, f) for f in range(3)]
         scale = jnp.concatenate([jnp.broadcast_to(flag.astype(F32), tile_shape) for flag in has], 0)
         halo = [jnp.where(scale > 0.0, stack(hb, k, f), own) for f, own in enumerate(mine)]
@@ -433,9 +455,8 @@
 
         @pl.when(k == 0)
         def _():
-            wait_arrived(eps_copies(), has, OPPOSITE)
             for s in range(4):
-                wb[s] = keep(has[s], se[s] + hex_[s])
+                wb[s] = keep(has[s], sb[0, s, EPS_AT:EPS_AT + SIDE, :] + hb[0, s, EPS_AT:EPS_AT + SIDE, :])
                 fc[border[s], :] = fc[border[s], :] + wb[s]
             for s in range(4):
                 fcb[s] = fc[border[s], :]
@@ -458,13 +479,13 @@
                 new = []
                 for s in pair:
                     new.append(newton(
-                        [sb[k, s, f] for f in range(3)], [acc[q, border[s], :] for q in range(7)],
+                        [sb[k, s, SIDE * f:SIDE * f + SIDE, :] for f in range(3)], [acc[q, border[s], :] for q in range(7)],
                         fcb[s], mobb[s], dopb[s], eleb[s] == 1,
                     ))
                 for s, values in zip(pair, new):
                     for f in range(3):
-                        sb[following, s, f] = values[f]
-                start(state_copies(following), has, pair)
+                        sb[following, s, SIDE * f:SIDE * f + SIDE, :] = values[f]
+                start_state(state_copies(following), pair)
 
         for c in range(CELLS):
             for y in range(CELLS):
@@ -472,14 +493,12 @@
 
         @pl.when(k == 0)
         def _():
-            wait_sent(eps_copies(), has)
-            wait_sent(cond_copies(), has)
-            wait_arrived(cond_copies(), has, OPPOSITE)
-            cx[1, 0:2, :] = keep(has[0], cr[0, 2:4, :])
-            cx[1, 2:6, :] = cs[0:4, :]
-            cx[1, 6:8, :] = keep(has[1], cr[1, 0:2, :])
-            cx[0, 2:6, :] = keep(has[2], cr[2, 0:4, :])
-            cx[2, 2:6, :] = keep(has[3], cr[3, 0:4, :])
+            at = COND_AT
+            cx[1, 0:2, :] = keep(has[0], hb[0, 0, at + 2:at + 4, :])
+            cx[1, 2:6, :] = sb[0, 0, at:at + 4, :]
+            cx[1, 6:8, :] = keep(has[1], hb[0, 1, at:at + 2, :])
+            cx[0, 2:6, :] = keep(has[2], hb[0, 2, at:at + 4, :])
+            cx[2, 2:6, :] = keep(has[3], hb[0, 3, at:at + 4, :])
 
         def solve(x, nothing):
             rows = slab(x)
@@ -493,7 +512,13 @@
             return nothing
 
         lax.fori_loop(0, SIDE, solve, 0)
-        wait_sent(state_copies(k), has)
+        @pl.when(k == 0)
+        def _():
+            wait_sent(first_copies(), has)
+
+        @pl.when(k > 0)
+        def _():
+            wait_sent(state_copies(k), has)
 
         @pl.when(k > 0)
         def _():
@@ -563,12 +588,8 @@
                 vm((48, LANES), F32),
                 vm((48, LANES // 4), F32),
                 vm((4,) + tile, F32),
-                vm((NEWTON, 4, 3) + tile, F32),
-                vm((4,) + tile, F32),
-                vm((4,) + tile, F32),
-                vm((NEWTON, 4, 3) + tile, F32),
-                vm((8, LANES), F32),
-                vm((4, 8, LANES), F32),
+                vm((NEWTON, 4, FIRST_ROWS, LANES), F32),
+                vm((NEWTON, 4, FIRST_ROWS, LANES), F32),
                 vm((NEWTON + 1, 8, LANES), F32),
                 vm((NEWTON + 1, 4, 2, LANES), F32),
                 vm((NEWTON + 1, 4, 8, LANES), F32),
@@ -581,10 +602,6 @@
                 dma((6,)),
                 dma((NEWTON, 4)),
                 dma((NEWTON, 4)),
-                dma((4,)),
-                dma((4,)),
-                dma((4,)),
-                dma((4,)),
                 dma((NEWTON + 1, 4)),
                 dma((NEWTON + 1, 4)),
                 dma((NEWTON + 1, 4)),

time: 36.1 us -> 34.8 us (0.964); the launches traced: 36 us -> 34.3 us
  Pallas kernels: 35.3 us -> 33.7 us
    pallas_call x1, Pallas kernels: 34.5 us -> 32.9 us  [per_device(): call(sol.reshape(3, NODES, LANES), ins.reshape(NODES, LANES), ele.reshape...]
where the time goes in v5:
time: 34.8 us; the launch traced here: 34.3 us
  Pallas kernels  33.7 us (97%)
  between operations  0.64 us (2%)
    pallas_call x1, Pallas kernels, per_device(): call(sol.reshape(3, NODES, LANES), ins.reshape(NODES, LANES), ele.reshape...  32.9 us
    pallas_call x1, Pallas kernels, per_device(): pl.pallas_call(emit, out_shape=(jax.ShapeDtypeStruct((3, NODES, LANES), F...  0.79 us

profile of v5, /device:TPU:15, one launch (start us, length us, event | category | flops | bytes accessed | tf_op | source)
XLA Modules:
  0.0 34.3 jit_solution(39408186959762111)
XLA Ops:
  0.6 32.9 %shard_map.77 = (f32[3,256,128]{2,1,0:T(8,128)S(1)}, f32[8,128]{1,0:T(8,128)S(1)}) custom-call(f32[3,256,128]{2,1,0:T(8,128)} %bitcast.4, s32[256,128]{1,0:T(8,128)} %bitcast.5, s32[256,128]{1,0:T(8,128)} %bitcast.6, s32[4,4,32]{2,1,0:T(4,128)} %imp_ref.1, s32[4,4,32]{2,1,0:T(4,128)} %con_ref.1, f32[4,4,32]{2,1,0:T(4,128)} %war_ref.1), custom_call_target="tpu_custom_call" | custom-call | tf_op jit(solution)/shard_map/pallas_call | solution.py:612
  33.5 0.8 %shard_map.78 = (f32[3,256,128]{2,1,0:T(8,128)}, f32[4,4,32]{2,1,0:T(4,128)}) custom-call(f32[3,256,128]{2,1,0:T(8,128)S(1)} %get-tuple-element.6.st_ref, f32[8,128]{1,0:T(8,128)S(1)} %get-tuple-element.7.warm_ref), custom_call_target="tpu_custom_call" | custom-call | tf_op jit(solution)/shard_map/pallas_call | solution.py:617
